TPU v7x, 32 devices: a whole 2x2x4 slice. The times are simulated.
32 devices in a mesh: freq: 2 (over x), atom: 16 (over z, y, core).
Axes of the slice: x: 2, y: 2, z: 4, core: 2. Of those that a mesh axis runs over, the one named last changes fastest.
Arguments:
- ham_diag: float32 [2, 128, 128], replicated
- ham_coup: float32 [1, 128, 128], replicated, may hold values from -0.25 to 0.25
- neighbors: int32 [256, 64], replicated, may hold values from 0 to 127, as said below
- pair_count: int32 [256], replicated, may hold values from 16 to 64
- shifts: int32 [8], replicated, may hold values from 1 to 16
- g_pairs: float32 [2, 32, 16384], P(None, ('freq', 'atom')), may hold values from -3 to 3
- emit_coup: float32 [2, 8, 16384], replicated, may hold values from -0.09375 to 0.09375
- absorb_coup: float32 [2, 8, 16384], replicated, may hold values from -0.09375 to 0.09375
Outputs:
- green: float32 [2, 32, 2, 128, 128], P(None, ('freq', 'atom'))
Inputs may be any that keep to these rules, and one draw needn't show every extreme that they name: `neighbors`: entry 0 of each row is the atom's own index within its slab (atom index modulo 128); the entries of a row are distinct.
All inputs are finite; a program needn't handle non-finite values.
Results may differ from a plain program's by a relative error of at most 0.0001.
Values sent between devices are 32-bit elements; how exact they have to be, the bound alone decides.
No kernel may reach another device: no remote copies, remote signals or barrier semaphores. Data moves between devices by JAX's collectives and lax.ppermute only.
A program may use at most 128 MiB of HBM per device.

v0:
```python
import jax
import jax.numpy as jnp
from jax import lax
from jax.sharding import PartitionSpec as P

ORB = 128
SLABS = 2
NBR = 64
MODES = 8
HALO = 16
INV_STEPS = 22


BROADEN = 0.8
ENERGY_LOW = -2.5
ENERGY_SPAN = 5.0


def with_halo(cells, sides, width):
    for axis, dim in sides:
        count = lax.axis_size(axis)
        ends = count - 1
        head = lax.slice_in_dim(cells, 0, width, axis=dim)
        tail = lax.slice_in_dim(cells, cells.shape[dim] - width, cells.shape[dim], axis=dim)
        cells = jnp.concatenate(
            [
                lax.ppermute(tail, axis, [(i, (i + 1) % count) for i in range(ends)]),
                cells,
                lax.ppermute(head, axis, [((i + 1) % count, i) for i in range(ends)]),
            ],
            axis=dim,
        )
    return cells


def matmul(left, right):
    return jnp.dot(left, right, precision=lax.Precision.HIGHEST, preferred_element_type=jnp.float32)


def complex_product(left, right):
    first = matmul(left[0], right[0])
    second = matmul(left[1], right[1])
    third = matmul(left[0] + left[1], right[0] + right[1])
    return (first - second, third - first - second)


def sandwich(outer_left, inner, outer_right):
    return (
        matmul(matmul(outer_left, inner[0]), outer_right),
        matmul(matmul(outer_left, inner[1]), outer_right),
    )


def invert(real_part, imag_part):
    order = real_part.shape[0]
    unit_matrix = jnp.eye(order, dtype=real_part.dtype)
    scale = 1.0 / (jnp.sum(real_part * real_part) + jnp.sum(imag_part * imag_part))
    start = (real_part.T * scale, -imag_part.T * scale)

    def newton_step(index, current):
        product = complex_product((real_part, imag_part), current)
        residue = (2.0 * unit_matrix - product[0], -product[1])
        return complex_product(current, residue)

    return lax.fori_loop(0, INV_STEPS, newton_step, start)


def slab_green(sigma_blocks, energy, ham_diag, ham_coup):
    slabs = ham_diag.shape[0]
    order = ham_diag.shape[1]
    unit_matrix = jnp.eye(order, dtype=ham_diag.dtype)
    diag_real = [
        energy * unit_matrix - ham_diag[slab_index] - sigma_blocks[0, slab_index]
        for slab_index in range(slabs)
    ]
    diag_imag = [BROADEN * unit_matrix - sigma_blocks[1, slab_index] for slab_index in range(slabs)]
    right_parts = [None] * slabs
    right_parts[slabs - 1] = invert(diag_real[slabs - 1], diag_imag[slabs - 1])
    slab_index = 0
    coupling = ham_coup[slab_index]
    folded = sandwich(coupling, right_parts[slab_index + 1], coupling.T)
    right_parts[slab_index] = invert(
        diag_real[slab_index] - folded[0], diag_imag[slab_index] - folded[1]
    )
    blocks = [right_parts[0]]
    slab_index = 1
    coupling = ham_coup[slab_index - 1]
    carried = sandwich(coupling.T, blocks[-1], coupling)
    own_part = right_parts[slab_index]
    update = complex_product(complex_product(own_part, carried), own_part)
    blocks.append((own_part[0] + update[0], own_part[1] + update[1]))
    return jnp.stack(
        [jnp.stack([entry[0] for entry in blocks]), jnp.stack([entry[1] for entry in blocks])]
    )


def sigma_blocks_of(sigma_pairs, neighbors, live):
    values = sigma_pairs.reshape(2, SLABS, ORB, NBR) * live
    slab_ids = jnp.broadcast_to(
        jnp.arange(SLABS, dtype=jnp.int32)[:, None, None], (SLABS, ORB, NBR)
    )
    row_ids = jnp.broadcast_to(jnp.arange(ORB, dtype=jnp.int32)[None, :, None], (SLABS, ORB, NBR))
    columns = neighbors.reshape(SLABS, ORB, NBR)
    empty = jnp.zeros((2, SLABS, ORB, ORB), sigma_pairs.dtype)
    return empty.at[:, slab_ids, row_ids, columns].add(values)


def convolve(source, base, length, shifts, emit_coup, absorb_coup):
    width = source.shape[2]
    real_sum = jnp.zeros((length, width), source.dtype)
    imag_sum = jnp.zeros((length, width), source.dtype)
    for mode_index in range(MODES):
        shift_now = shifts[mode_index]
        below = lax.dynamic_slice_in_dim(source, base - shift_now, length, 1)
        above = lax.dynamic_slice_in_dim(source, base + shift_now, length, 1)
        emit_real = emit_coup[0, mode_index][None, :]
        emit_imag = emit_coup[1, mode_index][None, :]
        absorb_real = absorb_coup[0, mode_index][None, :]
        absorb_imag = absorb_coup[1, mode_index][None, :]
        real_sum = (
            real_sum
            + emit_real * below[0]
            - emit_imag * below[1]
            + absorb_real * above[0]
            - absorb_imag * above[1]
        )
        imag_sum = (
            imag_sum
            + emit_real * below[1]
            + emit_imag * below[0]
            + absorb_real * above[1]
            + absorb_imag * above[0]
        )
    return jnp.stack([real_sum, imag_sum])


def on_device(ham_diag, ham_coup, neighbors, pair_count, shifts, g_pairs, emit_coup, absorb_coup):
    e_dev = g_pairs.shape[1]
    atom_count = lax.axis_size("atom")
    group = e_dev * atom_count
    energy_total = group * lax.axis_size("freq")
    freq_index = lax.axis_index("freq")
    atom_index = lax.axis_index("atom")
    live = (
        (jnp.arange(NBR, dtype=jnp.int32)[None, :] < pair_count[:, None])
        .astype(jnp.float32)
        .reshape(SLABS, ORB, NBR)
    )
    first_energy = (freq_index * atom_count + atom_index) * e_dev

    def solve_one(sigma_pairs, energy):
        return slab_green(sigma_blocks_of(sigma_pairs, neighbors, live), energy, ham_diag, ham_coup)

    owned = lax.all_to_all(g_pairs, "atom", split_axis=2, concat_axis=1, tiled=True)
    owned_width = owned.shape[2]
    own_emit = lax.dynamic_slice_in_dim(emit_coup, atom_index * owned_width, owned_width, 2)
    own_absorb = lax.dynamic_slice_in_dim(absorb_coup, atom_index * owned_width, owned_width, 2)
    source = with_halo(owned, (("freq", 1),), HALO)
    sigma = convolve(source, HALO, group, shifts, own_emit, own_absorb)
    returned = lax.all_to_all(sigma, "atom", split_axis=1, concat_axis=2, tiled=True)

    def single(pieces):
        return solve_one(pieces[0], pieces[1])

    positions = (first_energy + jnp.arange(e_dev, dtype=jnp.int32)).astype(jnp.float32)
    solved = lax.map(
        single, (jnp.moveaxis(returned, 1, 0), ENERGY_LOW + ENERGY_SPAN * positions / energy_total)
    )
    return jnp.moveaxis(solved, 0, 1)


def solution(mesh):
    return jax.shard_map(
        on_device,
        mesh=mesh,
        in_specs=(P(), P(), P(), P(), P(), P(None, ("freq", "atom"), None), P(), P()),
        out_specs=P(None, ("freq", "atom"), None, None, None),
        check_vma=False,
    )
```

profile of v0, /device:TPU:0, one launch (start us, length us, event | category | flops | bytes accessed | tf_op | source)
XLA Modules:
  0.0 409.6 jit_solution(11434350478482396900)
XLA Ops:
  0.0 14.7 %copy.80 = f32[2,1,16384]{0,1,2:T(1,128)} copy(f32[2,1,16384]{2,1,0:T(1,128)} %param.17) | data formatting | bytes 262144 | tf_op args[5]
  14.7 0.5 broadcast.412
  15.2 74.4 %reduce.4 = f32[16384,2]{1,0:T(8,128)} reduce(f32[16384,1,2]{2,1,0:T(1,128)} %bitcast.233, f32[]{:T(128)} %broadcast.412), dimensions={1}, to_apply=%bitcast.153.reduce_sub_computation | reduce | bytes 262148
  89.6 8.3 %reshape.561 = f32[16,1,2048]{2,1,0:T(1,128)} reshape(f32[16384,2]{1,0:T(8,128)} %reduce.4) | data formatting | bytes 262144
  97.9 7.4 %all-to-all-start = ((f32[16,1,2048]{2,1,0:T(1,128)}), f32[16,1,2048]{2,1,0:T(1,128)S(1)}, u32[]{:S(2)}, u32[]{:S(2)}) async-start(f32[16,1,2048]{2,1,0:T(1,128)} %reshape.561), calls=%async_computation | async-start | bytes 262144 | tf_op jit(solution)/shard_map/all_to_all | solution.py:154
  105.3 0.7 fusion.62
  126.2 2.0 constant_dynamic-slice_fusion.1
  128.6 0.9 reduce.5
  129.4 14.7 %reshape.562 = f32[16384,1,2]{2,1,0:T(1,128)} reshape(f32[16,2048]{1,0:T(8,128)S(1)} %reduce.5) | data formatting | bytes 262144
  144.2 5.2 %copy.95 = f32[2,16,1024]{2,1,0:T(8,128)S(1)} copy(f32[2,16,1024]{0,2,1:T(8,128)} %bitcast.234) | data formatting | bytes 262144 | tf_op jit(solution)/shard_map/all_to_all | solution.py:154
  149.4 1.3 collective-permute-start.1
  150.7 4.6 %collective-permute-start = (f32[2,16,1024]{2,1,0:T(8,128)S(1)}, f32[2,16,1024]{2,1,0:T(8,128)S(1)}, u32[]{:S(2)}, u32[]{:S(2)}) collective-permute-start(f32[2,16,1024]{2,1,0:T(8,128)S(1)} %copy.95), channel_id=1, source_target_pairs={{0,16},{1,17},{2,18},{3,19},{4,20},{5,21},{6,22},{7,23},{8,24},{9,... | collective-permute-start | bytes 393224 | tf_op jit(solution)/shard_map/ppermute | solution.py:27
  155.5 1.7 collective-permute-done.1
  157.2 1.2 collective-permute-done
  158.4 0.6 multiply_subtract_fusion
  159.0 0.6 multiply_add_fusion
  159.6 0.8 copy.82
  160.4 5.8 %all-to-all-start.1 = ((f32[2,16,1024]{2,0,1:T(2,128)}), f32[2,16,1024]{2,0,1:T(2,128)S(1)}, u32[]{:S(2)}, u32[]{:S(2)}) async-start(f32[2,16,1024]{2,0,1:T(2,128)} %copy.82), calls=%async_computation.1 | async-start | bytes 262144 | tf_op jit(solution)/shard_map/all_to_all | solution.py:160
  166.5 7.5 %all-to-all-done.1 = f32[2,16,1024]{2,0,1:T(2,128)S(1)} async-done(((f32[2,16,1024]{2,0,1:T(2,128)}), f32[2,16,1024]{2,0,1:T(2,128)S(1)}, u32[]{:S(2)}, u32[]{:S(2)}) %all-to-all-start.1) | async-done | bytes 131104 | tf_op jit(solution)/shard_map/all_to_all | solution.py:160
  174.2 4.8 %copy.96 = f32[2,128,64,2]{3,2,1,0:T(8,128)} copy(f32[2,128,64,2]{2,1,0,3:T(8,128)S(1)} %multiply_bitcast_fusion) | data formatting | bytes 262144 | tf_op jit(solution)/shard_map/while/body/eval_jaxpr/mul | solution.py:98
  179.0 94.4 %scatter_custom_fusion = f32[2,32768]{0,1:T(8,128)} fusion(s32[16384]{0:T(1024)S(1)} %reshape.553, f32[16384,2]{1,0:T(8,128)} %bitcast.235, f32[]{:T(128)} %constant.119.clone.1), kind=kCustom, calls=%fused_computation.37 | custom fusion | flops 32768 | bytes 262656
  273.4 27.8 %fusion.60 = (f32[1,1,128,128]{0,3,2,1:T(8,128)}, f32[1,1,128,128]{0,3,2,1:T(8,128)}, f32[1,1,128,128]{0,3,2,1:T(8,128)}, f32[1,1,128,128]{0,3,2,1:T(8,128)}) fusion(f32[2,2,128,128]{0,3,2,1:T(8,128)} %bitcast.232), kind=kLoop, calls=%fused_computation.120 | loop fusion | bytes 524288 | tf_op jit(solution)/shard_map/while/body/eval_jaxpr/slice | solution.py:76
  301.2 5.2 %copy.100 = f32[1,1,128,128]{3,2,1,0:T(8,128)S(1)} copy(f32[1,1,128,128]{0,3,2,1:T(8,128)} %get-tuple-element.218) | data formatting | bytes 131072
  306.4 5.2 %copy.99 = f32[1,1,128,128]{3,2,1,0:T(8,128)S(1)} copy(f32[1,1,128,128]{0,3,2,1:T(8,128)} %get-tuple-element.219) | data formatting | bytes 131072
  311.6 0.6 select_subtract_fusion.7
  312.3 0.7 multiply_reduce_fusion.4
  314.4 38.5 %while.40 = (s32[]{:T(128)}, f32[128,128]{0,1:T(8,128)S(1)}, f32[128,128]{0,1:T(8,128)S(1)}, f32[128,128]{1,0:T(8,128)S(1)}, f32[128,128]{1,0:T(8,128)S(1)}, /*index=5*/f32[128,128]{1,0:T(8,128)S(1)}, s32[]{:T(128)}) while((s32[]{:T(128)}, f32[128,128]{0,1:T(8,128)S(1)}, f32[128,128]{0,1:T(8,128)S(1)}, f32[128,128]{1,0:T(8,128)S(1)}, ...), condition=%wide.region_4.5_spmd.clone, body=%wide.region_3.4_spmd.clone.sunk | while | flops 151273472 | bytes 2162765 | solution.py:65
  319.3 0.3 fusion.148
  321.1 0.3 fusion.148
  322.8 0.3 fusion.148
  324.6 0.3 fusion.148
  326.3 0.3 fusion.148
  328.1 0.3 fusion.148
  329.8 0.3 fusion.148
  331.6 0.3 fusion.148
  333.3 0.3 fusion.148
  335.1 0.3 fusion.148
  336.8 0.3 fusion.148
  338.6 0.3 fusion.148
  340.3 0.3 fusion.148
  342.1 0.3 fusion.148
  352.6 0.3 fusion.148
  353.7 5.2 %copy.101 = f32[1,1,128,128]{3,2,1,0:T(8,128)S(1)} copy(f32[1,1,128,128]{0,3,2,1:T(8,128)} %get-tuple-element.217) | data formatting | bytes 131072
  358.9 5.2 %copy.98 = f32[1,1,128,128]{3,2,1,0:T(8,128)S(1)} copy(f32[1,1,128,128]{0,3,2,1:T(8,128)} %get-tuple-element.220) | data formatting | bytes 131072
  364.1 1.0 multiply_reduce_fusion.1
  365.1 0.9 multiply_reduce_fusion.2
  367.4 38.5 %while.41 = (s32[]{:T(128)}, f32[128,128]{0,1:T(8,128)S(1)}, f32[128,128]{0,1:T(8,128)S(1)}, f32[128,128]{1,0:T(8,128)S(1)}, f32[128,128]{1,0:T(8,128)S(1)}, /*index=5*/f32[128,128]{1,0:T(8,128)S(1)}, s32[]{:T(128)}) while((s32[]{:T(128)}, f32[128,128]{0,1:T(8,128)S(1)}, f32[128,128]{0,1:T(8,128)S(1)}, f32[128,128]{1,0:T(8,128)S(1)}, ...), condition=%wide.region_8.9_spmd.clone, body=%wide.region_7.8_spmd.clone.sunk | while | flops 151273472 | bytes 2162765 | solution.py:65
  408.9 0.7 maximum_bitcast_fusion
  (389 shorter events, 74.9 us)
Async XLA Ops:
  0.0 353.0 %copy-start = (f32[1,128,128]{2,1,0:T(8,128)S(1)}, f32[1,128,128]{2,1,0:T(8,128)}, u32[]{:S(2)}) copy-start(f32[1,128,128]{2,1,0:T(8,128)} %param.13) | copy-start | bytes 196612
  89.6 15.7 %copy-start.3 = (s32[8]{0:T(128)S(1)}, s32[8]{0:T(128)}, u32[]{:S(2)}) copy-start(s32[8]{0:T(128)} %param.16) | copy-start | bytes 100
  89.6 36.4 %copy-start.2 = (s32[256,64]{0,1:T(8,128)S(1)}, s32[256,64]{0,1:T(8,128)}, u32[]{:S(2)}) copy-start(s32[256,64]{0,1:T(8,128)} %param.14) | copy-start | bytes 196612
  89.6 38.7 %copy-start.6 = (s32[3]{0:T(128)S(1)}, s32[3]{0:T(128)}, u32[]{:S(2)}) copy-start(s32[3]{0:T(128)} %constant.131) | copy-start | bytes 40
  97.9 30.7 %all-to-all-start = ((f32[16,1,2048]{2,1,0:T(1,128)}), f32[16,1,2048]{2,1,0:T(1,128)S(1)}, u32[]{:S(2)}, u32[]{:S(2)}) async-start(f32[16,1,2048]{2,1,0:T(1,128)} %reshape.561), calls=%async_computation | async-start | bytes 262144 | tf_op jit(solution)/shard_map/all_to_all | solution.py:154
  129.4 25.9 %copy-start.5 = (s32[3]{0:T(128)S(1)}, s32[3]{0:T(128)}, u32[]{:S(2)}) copy-start(s32[3]{0:T(128)} %constant.128) | copy-start | bytes 40
  144.2 22.2 %copy-start.4 = (s32[256]{0:T(256)S(1)}, s32[256]{0:T(256)}, u32[]{:S(2)}) copy-start(s32[256]{0:T(256)} %param.15) | copy-start | bytes 3076
  149.4 7.7 %collective-permute-start.1 = (f32[2,16,1024]{2,1,0:T(8,128)S(1)}, f32[2,16,1024]{2,1,0:T(8,128)S(1)}, u32[]{:S(2)}, u32[]{:S(2)}) collective-permute-start(f32[2,16,1024]{2,1,0:T(8,128)S(1)} %copy.95), channel_id=1, source_target_pairs={{16,0},{17,1},{18,2},{19,3},{20,4},{21,5},{22,6},{23,7},{24,8},{25... | collective-permute-start | bytes 393224 | tf_op jit(solution)/shard_map/ppermute | solution.py:29
  150.7 7.6 %collective-permute-start = (f32[2,16,1024]{2,1,0:T(8,128)S(1)}, f32[2,16,1024]{2,1,0:T(8,128)S(1)}, u32[]{:S(2)}, u32[]{:S(2)}) collective-permute-start(f32[2,16,1024]{2,1,0:T(8,128)S(1)} %copy.95), channel_id=1, source_target_pairs={{0,16},{1,17},{2,18},{3,19},{4,20},{5,21},{6,22},{7,23},{8,24},{9,... | collective-permute-start | bytes 393224 | tf_op jit(solution)/shard_map/ppermute | solution.py:27
  160.4 13.7 %all-to-all-start.1 = ((f32[2,16,1024]{2,0,1:T(2,128)}), f32[2,16,1024]{2,0,1:T(2,128)S(1)}, u32[]{:S(2)}, u32[]{:S(2)}) async-start(f32[2,16,1024]{2,0,1:T(2,128)} %copy.82), calls=%async_computation.1 | async-start | bytes 262144 | tf_op jit(solution)/shard_map/all_to_all | solution.py:160
  301.2 10.5 %copy-start.1 = (f32[2,128,128]{2,1,0:T(8,128)S(1)}, f32[2,128,128]{2,1,0:T(8,128)}, u32[]{:S(2)}) copy-start(f32[2,128,128]{2,1,0:T(8,128)} %param.12) | copy-start | bytes 393220
where the time goes:
time: 412 us; the launch traced here: 410 us
  other arithmetic  174 us (42%)
  local copies, waits for them, and re-layouts  102 us (25%)
  matrix products  79.1 us (19%)
  between operations  23.3 us (6%)
  starting transfers between devices  19 us (5%)
  waiting for transfers between devices  10.4 us (3%)
    unnamed x5, other arithmetic  169 us
    dot_general x278, matrix products, matmul(): jnp.dot(left, right, precision=lax.Precision.HIGHEST, preferred_element_t...  79.1 us
    unnamed x24, local copies, waits for them, and re-layouts  59.3 us
    slice x1, local copies, waits for them, and re-layouts, slab_green(): sigma_blocks[1, slab_index]  27.8 us
  transfers between devices with their start and end apart: 4, of which 3 were waited for; matrix products, arithmetic and copies ran while one was open for 1% of the time, Pallas kernels for 0%

commit v1 on v0

v1 whole, which is shorter than its diff:
```python
import functools

import jax
import jax.numpy as jnp
from jax import lax
from jax.experimental import pallas as pl
from jax.experimental.pallas import tpu as pltpu
from jax.sharding import PartitionSpec as P

HALO = 16
INV_STEPS = 22
EXACT_STEPS = 2

BROADEN = 0.8
ENERGY_LOW = -2.5
ENERGY_SPAN = 5.0

LANES = 128
RESIDUAL_LIMIT = 1e-4

AXES = ("freq", "atom")
VMEM = pltpu.MemorySpace.VMEM
SMEM = pltpu.MemorySpace.SMEM


def prepare_kernel(own_ref, neighbors_ref, count_ref, emit_ref, absorb_ref, table_ref, coef_ref):
    slabs, order, _ = table_ref.shape
    slots = neighbors_ref.shape[1]
    half = coef_ref.shape[3] // 2
    slot_id = lax.broadcasted_iota(jnp.int32, (slots, order), 0)
    column = lax.broadcasted_iota(jnp.int32, (order, order), 0)
    lane = lax.broadcasted_iota(jnp.int32, (order, order), 1)
    offset = lax.rem(lane, LANES // slots) * slots
    for slab in range(slabs):
        listed = neighbors_ref[slab * order : (slab + 1) * order, :].T
        listed = jnp.where(slot_id < count_ref[slab : slab + 1, :], listed, -1)
        found = jnp.full((order, order), -1, jnp.int32)
        for slot in range(slots):
            found = jnp.where(listed[slot : slot + 1, :] == column, slot, found)
        table_ref[slab] = jnp.where(found >= 0, found + offset, -1).T
    for side, weights_ref in enumerate((emit_ref, absorb_ref)):
        for row in range(half):
            lanes = slice(row * LANES, (row + 1) * LANES)
            real = weights_ref[0, :, lanes]
            imag = weights_ref[1, :, lanes]
            coef_ref[side, 0, :, row, :] = real
            coef_ref[side, 0, :, half + row, :] = real
            coef_ref[side, 1, :, row, :] = -imag
            coef_ref[side, 1, :, half + row, :] = imag


def prepare(own, neighbors, pair_count, emit_coup, absorb_coup, slabs, order, rows_per):
    modes = emit_coup.shape[1]
    blocks = emit_coup.shape[2] // (rows_per * LANES)
    weights = pl.BlockSpec(
        (2, modes, rows_per * LANES),
        lambda i, own_ref: (0, 0, jnp.minimum(own_ref[0], blocks - 1)),
    )
    whole = lambda *shape: pl.BlockSpec(shape, lambda i, own_ref: (0,) * len(shape))
    return pl.pallas_call(
        prepare_kernel,
        out_shape=(
            jax.ShapeDtypeStruct((slabs, order, order), jnp.int32),
            jax.ShapeDtypeStruct((2, 2, modes, 2 * rows_per, LANES), jnp.float32),
        ),
        grid_spec=pltpu.PrefetchScalarGridSpec(
            num_scalar_prefetch=1,
            grid=(1,),
            in_specs=[
                whole(*neighbors.shape),
                whole(slabs, order),
                weights,
                weights,
            ],
            out_specs=(
                whole(slabs, order, order),
                whole(2, 2, modes, 2 * rows_per, LANES),
            ),
        ),
        name="prepare",
    )(own, neighbors, pair_count.reshape(slabs, order), emit_coup, absorb_coup)


def convolve_kernel(shifts_ref, cells_ref, coef_ref, out_ref, plain_ref, swapped_ref):
    energies, height, _ = cells_ref.shape
    modes = coef_ref.shape[2]
    edge = jnp.zeros((HALO, height, LANES), jnp.float32)
    for ref in (plain_ref, swapped_ref):
        ref[0:HALO] = edge
        ref[HALO + energies : 2 * HALO + energies] = edge
    group = 32 if energies % 32 == 0 else 1

    def load(index, carry):
        for step in range(group):
            energy = index * group + step
            cell = cells_ref[energy]
            plain_ref[HALO + energy] = cell
            swapped_ref[HALO + energy] = jnp.concatenate(
                [cell[height // 2 :], cell[: height // 2]], axis=0
            )
        return carry

    def combine(index, carry):
        base = HALO + index * group
        total = [jnp.zeros((height, LANES), jnp.float32)] * group
        for mode in range(modes):
            shift = shifts_ref[mode]
            for side in range(2):
                first = base + (shift if side else -shift)
                direct = coef_ref[side, 0, mode]
                crossed = coef_ref[side, 1, mode]
                for step in range(group):
                    total[step] = (
                        total[step]
                        + direct * plain_ref[first + step]
                        + crossed * swapped_ref[first + step]
                    )
        for step in range(group):
            out_ref[index * group + step] = total[step]
        return carry

    lax.fori_loop(0, energies // group, load, 0)
    lax.fori_loop(0, energies // group, combine, 0)


def convolve(shifts, cells, coef):
    energies, height, _ = cells.shape
    padded = pltpu.VMEM((energies + 2 * HALO, height, LANES), jnp.float32)
    return pl.pallas_call(
        convolve_kernel,
        out_shape=jax.ShapeDtypeStruct(cells.shape, jnp.float32),
        in_specs=[
            pl.BlockSpec(memory_space=SMEM),
            pl.BlockSpec(memory_space=VMEM),
            pl.BlockSpec(memory_space=VMEM),
        ],
        out_specs=pl.BlockSpec(memory_space=VMEM),
        scratch_shapes=[padded, padded],
        name="convolve",
    )(shifts, cells, coef)


def embed(pair):
    order = pair.shape[1] // 2
    return jnp.concatenate(
        [pair, jnp.concatenate([-pair[:, order:], pair[:, :order]], axis=1)], axis=0
    )


def full_dot(left, right):
    return jnp.dot(left, right, precision=lax.Precision.HIGHEST, preferred_element_type=jnp.float32)


def narrow_dot(left, right):
    return jnp.dot(
        left.astype(jnp.bfloat16), right.astype(jnp.bfloat16), preferred_element_type=jnp.float32
    )


def halves(pair):
    order = pair.shape[1] // 2
    return pair[:, :order], pair[:, order:]


def pair_of(real, imag):
    return jnp.concatenate([real, imag], axis=1)


def unit_pair(order):
    row = lax.broadcasted_iota(jnp.int32, (order, 2 * order), 0)
    column = lax.broadcasted_iota(jnp.int32, (order, 2 * order), 1)
    return jnp.where(row == column, 1.0, 0.0).astype(jnp.float32)


def start_of(matrix):
    real, imag = halves(matrix)
    scale = 1.0 / jnp.sum(matrix * matrix)
    return pair_of(real.T * scale, imag.T * -scale)


def invert(matrix, state_ref):
    order = matrix.shape[0]
    start = start_of(matrix)
    state_ref[:order] = start
    state_ref[order:] = full_dot(matrix, embed(start))

    def step(index, carry):
        state = state_ref[...]
        narrow = state.astype(jnp.bfloat16)
        product = jnp.dot(narrow, embed(narrow[order:]), preferred_element_type=jnp.float32)
        state_ref[...] = (state - product) + state
        return carry

    lax.fori_loop(0, INV_STEPS - EXACT_STEPS, step, 0)
    current = state_ref[:order]
    unit = unit_pair(order)
    for _ in range(EXACT_STEPS):
        residual = unit - full_dot(matrix, embed(current))
        current = current + narrow_dot(current, embed(residual))
    return current, jnp.sum(residual * residual)


def invert_plain(matrix):
    unit = unit_pair(matrix.shape[0])

    def step(index, current):
        residue = 2.0 * unit - full_dot(matrix, embed(current))
        return full_dot(current, embed(residue))

    return lax.fori_loop(0, INV_STEPS, step, start_of(matrix))


def solve_kernel(own_ref, cells_ref, table_ref, diag_ref, coup_ref, out_ref, matrix_ref, state_ref, *, energies):
    slabs, order, _ = diag_ref.shape
    unit = unit_pair(order)
    position = jnp.full((8, LANES), own_ref[0], jnp.int32).astype(jnp.float32)
    energy = (ENERGY_LOW + ENERGY_SPAN * position / energies)[0:1, 0:1]
    row = lax.broadcasted_iota(jnp.int32, (8, LANES), 0)
    lines = cells_ref.shape[1] // 2
    line_of = row // (8 // lines)
    for slab in range(slabs):
        for block in range(order // 8):
            cell = cells_ref[slab * (order // 8) + block]
            rows = slice(block * 8, block * 8 + 8)
            table = table_ref[slab, rows, :]
            held = table >= 0
            lane = jnp.where(held, table, 0)
            for part in range(2):
                spread = jnp.take_along_axis(cell, line_of + part * lines, axis=0)
                sigma = jnp.where(held, jnp.take_along_axis(spread, lane, axis=1), 0.0)
                eye = unit[rows, :order]
                if part == 0:
                    entry = energy * eye - diag_ref[slab, rows, :] - sigma
                else:
                    entry = BROADEN * eye - sigma
                matrix_ref[slab, rows, part * order : (part + 1) * order] = entry

    coup = coup_ref[0]
    coup_t = coup.T

    def right_by(pair, other):
        real, imag = halves(pair)
        return pair_of(full_dot(real, other), full_dot(imag, other))

    def finish(invert_one):
        last, last_norm = invert_one(matrix_ref[1])
        left_of = full_dot(coup, last)
        right_of = right_by(last, coup_t)
        first, first_norm = invert_one(matrix_ref[0] - right_by(left_of, coup_t))
        update = full_dot(full_dot(right_of, embed(first)), embed(left_of))
        second = last + update
        for part in range(2):
            columns = slice(part * order, (part + 1) * order)
            out_ref[part, 0] = first[:, columns]
            out_ref[part, 1] = second[:, columns]
        return jnp.maximum(last_norm, first_norm), last_norm + first_norm

    worst, total = finish(lambda matrix: invert(matrix, state_ref))
    settled = jnp.logical_and(worst <= RESIDUAL_LIMIT, total == total)

    @pl.when(jnp.logical_not(settled))
    def _():
        finish(lambda matrix: (invert_plain(matrix), jnp.float32(0.0)))


def solve(own, cells, table, ham_diag, ham_coup, energies):
    slabs, order, _ = ham_diag.shape
    vmem = pl.BlockSpec(memory_space=VMEM)
    return pl.pallas_call(
        functools.partial(solve_kernel, energies=energies),
        out_shape=jax.ShapeDtypeStruct((2, slabs, order, order), jnp.float32),
        in_specs=[pl.BlockSpec(memory_space=SMEM), vmem, vmem, vmem, vmem],
        out_specs=vmem,
        scratch_shapes=[
            pltpu.VMEM((slabs, order, 2 * order), jnp.float32),
            pltpu.VMEM((2 * order, 2 * order), jnp.float32),
        ],
        name="solve",
    )(own, cells, table, ham_diag, ham_coup)


def on_device(ham_diag, ham_coup, neighbors, pair_count, shifts, g_pairs, emit_coup, absorb_coup):
    slabs, order, _ = ham_diag.shape
    atoms, slots = neighbors.shape
    devices = lax.axis_size("freq") * lax.axis_size("atom")
    own = (lax.axis_index("freq") * lax.axis_size("atom") + lax.axis_index("atom")).astype(jnp.int32).reshape(1)
    rows = g_pairs.shape[2] // LANES
    rows_per = -(-rows // devices)
    spare = rows_per * devices - rows

    cells = g_pairs.reshape(2, rows, LANES)
    if spare:
        cells = jnp.pad(cells, ((0, 0), (0, spare), (0, 0)))
    cells = cells.reshape(2, devices, rows_per, LANES).transpose(1, 0, 2, 3)
    cells = cells.reshape(devices, 2 * rows_per, LANES)
    owned = lax.all_to_all(cells, AXES, 0, 0, tiled=True)
    table, coef = prepare(own, neighbors, pair_count, emit_coup, absorb_coup, slabs, order, rows_per)
    sigma = convolve(shifts, owned, coef)
    sigma = lax.all_to_all(sigma, AXES, 0, 0, tiled=True)
    lines = 8 * slots // LANES
    if rows_per != lines:
        sigma = sigma.reshape(devices, 2, rows_per, LANES).transpose(1, 0, 2, 3)
        sigma = sigma.reshape(2, devices * rows_per, LANES)[:, :rows]
        sigma = sigma.reshape(2, rows // lines, lines, LANES).transpose(1, 0, 2, 3)
        sigma = sigma.reshape(rows // lines, 2 * lines, LANES)
    green = solve(own, sigma, table, ham_diag, ham_coup, devices)
    return green.reshape(2, 1, slabs, order, order)


def solution(mesh):
    return jax.shard_map(
        on_device,
        mesh=mesh,
        in_specs=(P(), P(), P(), P(), P(), P(None, ("freq", "atom"), None), P(), P()),
        out_specs=P(None, ("freq", "atom"), None, None, None),
        check_vma=False,
    )
```

time: 412 us -> 45.6 us (0.11)
  other arithmetic: 174 us -> 0 us
  local copies, waits for them, and re-layouts: 102 us -> 2.99 us
  matrix products: 79.1 us -> 0 us
  between operations: 23.3 us -> 0.03 us
  Pallas kernels: 0 us -> 18.7 us
  starting transfers between devices: 19 us -> 7.33 us
  blocking collectives: 0 us -> 11.5 us
  waiting for transfers between devices: 10.4 us -> 4.82 us
    unnamed x5 -> x0, other arithmetic: 169 us -> none
    dot_general x278 -> x0, matrix products: 79.1 us -> none  [matmul(): jnp.dot(left, right, precision=lax.Precision.HIGHEST, preferred_element_t...]
    unnamed x24 -> x5, local copies, waits for them, and re-layouts: 59.3 us -> 1.41 us
    slice x3 -> x0, local copies, waits for them, and re-layouts: 30.4 us -> none  [the longest x1 27.8 us: slab_green(): sigma_blocks[1, slab_index]]
    pallas_call x0 -> x3, Pallas kernels: none -> 18.7 us  [the longest x1 14 us: solve(): pl.pallas_call(functools.partial(solve_kernel, energies=energies), out_sh...]
    all_to_all x0 -> x1, blocking collectives: none -> 11.5 us  [on_device(): sigma = lax.all_to_all(sigma, AXES, 0, 0, tiled=True)]
    all_to_all x2 -> x1, starting transfers between devices: 13.2 us -> 7.33 us  [on_device(): owned = lax.all_to_all(cells, AXES, 0, 0, tiled=True)]
    ppermute x2 -> x0, starting transfers between devices: 5.85 us -> none  [the longest x1 4.56 us: with_halo(): lax.ppermute(tail, axis, [(i, (i + 1) % count) for i in range(ends)])]
  transfers between devices with their start and end apart: 4 -> 1, of which waited for: 3 -> 1; matrix products, arithmetic and copies ran while one was open for 1% -> 2% of each run, Pallas kernels for 0% -> 6%
where the time goes in v1:
time: 45.6 us; the launch traced here: 45.3 us
  Pallas kernels  18.7 us (41%)
  blocking collectives  11.5 us (25%)
  starting transfers between devices  7.33 us (16%)
  waiting for transfers between devices  4.82 us (11%)
  local copies, waits for them, and re-layouts  2.99 us (7%)
    pallas_call x1, Pallas kernels, solve(): pl.pallas_call(functools.partial(solve_kernel, energies=energies), out_sh...  14 us
    all_to_all x1, blocking collectives, on_device(): sigma = lax.all_to_all(sigma, AXES, 0, 0, tiled=True)  11.5 us
    all_to_all x1, starting transfers between devices, on_device(): owned = lax.all_to_all(cells, AXES, 0, 0, tiled=True)  7.33 us
    all_to_all x1, waiting for transfers between devices, on_device(): owned = lax.all_to_all(cells, AXES, 0, 0, tiled=True)  4.82 us
    pallas_call x1, Pallas kernels, prepare(): pl.pallas_call(prepare_kernel, out_shape=(jax.ShapeDtypeStruct((slabs, or...  2.62 us
    pallas_call x1, Pallas kernels, convolve(): pl.pallas_call(convolve_kernel, out_shape=jax.ShapeDtypeStruct(cells.shap...  2.07 us
    another operation x1, local copies, waits for them, and re-layouts, on_device(): cells = cells.reshape(2, devices, rows_per, LANES).transpose(1, 0, 2, 3)  1.58 us
    unnamed x5, local copies, waits for them, and re-layouts  1.41 us
  transfers between devices with their start and end apart: 1, of which 1 were waited for; matrix products, arithmetic and copies ran while one was open for 2% of the time, Pallas kernels for 6%

profile of v1, /device:TPU:0, one launch (start us, length us, event | category | flops | bytes accessed | tf_op | source)
XLA Modules:
  0.0 45.3 jit_solution(8710658028732244963)
XLA Ops:
  0.0 1.6 %copy.9 = f32[2,32,4,128]{3,2,0,1:T(4,128)} copy(f32[2,32,4,128]{3,2,1,0:T(4,128)} %bitcast.9) | data formatting | bytes 262144 | tf_op jit(solution)/shard_map/reshape;reshape | solution.py:294
  1.6 0.0 copy-start.1
  1.6 7.3 %all-to-all-start = ((f32[32,8,128]{2,1,0:T(8,128)}), f32[32,8,128]{2,1,0:T(8,128)S(1)}, u32[]{:S(2)}, u32[]{:S(2)}) async-start(f32[32,8,128]{2,1,0:T(8,128)} %bitcast.3), calls=%async_computation | async-start | bytes 262144 | tf_op jit(solution)/shard_map/all_to_all | solution.py:296
  8.9 0.0 copy-done.1
  8.9 0.8 %copy.10.neighbors_ref = s32[256,64]{1,0:T(8,128)} copy(s32[256,64]{0,1:T(8,128)S(1)} %copy-done.1) | data formatting | bytes 131072 | tf_op args[2]
  9.7 2.6 %prepare.1 = (s32[2,128,128]{2,1,0:T(8,128)}, f32[2,2,8,8,128]{4,3,2,1,0:T(8,128)}) custom-call(s32[1]{0:T(128)} %bitcast.own_ref, s32[256,64]{1,0:T(8,128)} %copy.10.neighbors_ref, s32[2,128]{1,0:T(2,128)} %bitcast.10, f32[2,8,16384]{2,1,0:T(8,128)} %emit_ref.1, f32[2,8,16384]{2,1,0:T(8,128)} %absorb_ref.1), custom_call_target="tpu_custom_call" | custom-call | tf_op jit(solution)/shard_map/prepare/pallas_call | solution.py:60
  12.3 4.8 %all-to-all-done.cells_ref = f32[32,8,128]{2,1,0:T(8,128)S(1)} async-done(((f32[32,8,128]{2,1,0:T(8,128)}), f32[32,8,128]{2,1,0:T(8,128)S(1)}, u32[]{:S(2)}, u32[]{:S(2)}) %all-to-all-start) | async-done | bytes 131104 | tf_op jit(solution)/shard_map/all_to_all | solution.py:296
  17.1 0.0 copy-start
  17.1 0.7 %copy-done = f32[32,8,128]{2,1,0:T(8,128)} copy-done((f32[32,8,128]{2,1,0:T(8,128)}, f32[32,8,128]{2,1,0:T(8,128)S(1)}, u32[]{:S(2)}) %copy-start) | copy-done | bytes 131096
  17.8 2.1 %convolve.1 = f32[32,8,128]{2,1,0:T(8,128)} custom-call(s32[8]{0:T(128)} %shifts_ref.1, f32[32,8,128]{2,1,0:T(8,128)} %copy-done, f32[2,2,8,8,128]{4,3,2,1,0:T(8,128)} %get-tuple-element.7.coef_ref), custom_call_target="tpu_custom_call" | custom-call | tf_op jit(solution)/shard_map/convolve/pallas_call | solution.py:129
  19.8 11.5 %all_to_all.10.cells_ref = f32[32,8,128]{2,1,0:T(8,128)} all-to-all(f32[32,8,128]{2,1,0:T(8,128)} %convolve.1), channel_id=1, replica_groups=mesh['freq'=2,'atom'=16] {'freq','atom'}, dimensions={0} | all-to-all | bytes 262144 | tf_op jit(solution)/shard_map/all_to_all | solution.py:299
  31.3 14.0 %solve.1 = f32[2,2,128,128]{3,2,1,0:T(8,128)} custom-call(s32[1]{0:T(128)} %bitcast.own_ref, f32[32,8,128]{2,1,0:T(8,128)} %all_to_all.10.cells_ref, s32[2,128,128]{2,1,0:T(8,128)} %get-tuple-element.8.table_ref, f32[2,128,128]{2,1,0:T(8,128)} %diag_ref.1, f32[1,128,128]{2,1,0:T(8,128)} %coup_ref.1), custom_call_target="tpu_custom_call" | custom-call | tf_op jit(solution)/shard_map/solve/pallas_call | solution.py:269
Async XLA Ops:
  1.6 7.3 %copy-start.1 = (s32[256,64]{0,1:T(8,128)S(1)}, s32[256,64]{0,1:T(8,128)}, u32[]{:S(2)}) copy-start(s32[256,64]{0,1:T(8,128)} %param.10) | copy-start | bytes 196612
  1.6 15.5 %all-to-all-start = ((f32[32,8,128]{2,1,0:T(8,128)}), f32[32,8,128]{2,1,0:T(8,128)S(1)}, u32[]{:S(2)}, u32[]{:S(2)}) async-start(f32[32,8,128]{2,1,0:T(8,128)} %bitcast.3), calls=%async_computation | async-start | bytes 262144 | tf_op jit(solution)/shard_map/all_to_all | solution.py:296
  17.1 0.7 %copy-start = (f32[32,8,128]{2,1,0:T(8,128)}, f32[32,8,128]{2,1,0:T(8,128)S(1)}, u32[]{:S(2)}) copy-start(f32[32,8,128]{2,1,0:T(8,128)S(1)} %all-to-all-done.cells_ref) | copy-start | bytes 393220

commit v2 on v1

--- a/solution.py
+++ b/solution.py
@@ -77,6 +77,7 @@
                 whole(2, 2, modes, 2 * rows_per, LANES),
             ),
         ),
+        compiler_params=pltpu.CompilerParams(vmem_limit_bytes=16 * 2**20),
         name="prepare",
     )(own, neighbors, pair_count.reshape(slabs, order), emit_coup, absorb_coup)
 
@@ -136,6 +137,7 @@
         ],
         out_specs=pl.BlockSpec(memory_space=VMEM),
         scratch_shapes=[padded, padded],
+        compiler_params=pltpu.CompilerParams(vmem_limit_bytes=16 * 2**20),
         name="convolve",
     )(shifts, cells, coef)
 
@@ -275,6 +277,7 @@
             pltpu.VMEM((slabs, order, 2 * order), jnp.float32),
             pltpu.VMEM((2 * order, 2 * order), jnp.float32),
         ],
+        compiler_params=pltpu.CompilerParams(vmem_limit_bytes=16 * 2**20),
         name="solve",
     )(own, cells, table, ham_diag, ham_coup)
 

time: 45.6 us -> 42 us (0.921)
  Pallas kernels: 18.7 us -> 15 us
  local copies, waits for them, and re-layouts: 2.99 us -> 4.82 us
  blocking collectives: 11.5 us -> 10.5 us
  waiting for transfers between devices: 4.82 us -> 3.94 us
    unnamed x5 -> x15, local copies, waits for them, and re-layouts: 1.41 us -> 3.24 us
    pallas_call x1, Pallas kernels: 2.62 us -> 1 us  [prepare(): pl.pallas_call(prepare_kernel, out_shape=(jax.ShapeDtypeStruct((slabs, or...]
    pallas_call x1, Pallas kernels: 2.07 us -> 0.97 us  [convolve(): pl.pallas_call(convolve_kernel, out_shape=jax.ShapeDtypeStruct(cells.shap...]
    pallas_call x1, Pallas kernels: 14 us -> 13 us  [solve(): pl.pallas_call(functools.partial(solve_kernel, energies=energies), out_sh...]
    all_to_all x1, blocking collectives: 11.5 us -> 10.5 us  [on_device(): sigma = lax.all_to_all(sigma, AXES, 0, 0, tiled=True)]
    all_to_all x1, waiting for transfers between devices: 4.82 us -> 3.94 us  [on_device(): owned = lax.all_to_all(cells, AXES, 0, 0, tiled=True)]
  transfers between devices with their start and end apart: 1 -> 1, of which waited for: 1 -> 1; matrix products, arithmetic and copies ran while one was open for 2% -> 0% of each run, Pallas kernels for 6% -> 2%
where the time goes in v2:
time: 42 us; the launch traced here: 41.7 us
  Pallas kernels  15 us (36%)
  blocking collectives  10.5 us (25%)
  starting transfers between devices  7.33 us (17%)
  local copies, waits for them, and re-layouts  4.82 us (11%)
  waiting for transfers between devices  3.94 us (9%)
    pallas_call x1, Pallas kernels, solve(): pl.pallas_call(functools.partial(solve_kernel, energies=energies), out_sh...  13 us
    all_to_all x1, blocking collectives, on_device(): sigma = lax.all_to_all(sigma, AXES, 0, 0, tiled=True)  10.5 us
    all_to_all x1, starting transfers between devices, on_device(): owned = lax.all_to_all(cells, AXES, 0, 0, tiled=True)  7.33 us
    all_to_all x1, waiting for transfers between devices, on_device(): owned = lax.all_to_all(cells, AXES, 0, 0, tiled=True)  3.94 us
    unnamed x15, local copies, waits for them, and re-layouts  3.24 us
    another operation x1, local copies, waits for them, and re-layouts, on_device(): cells = cells.reshape(2, devices, rows_per, LANES).transpose(1, 0, 2, 3)  1.58 us
    pallas_call x1, Pallas kernels, prepare(): pl.pallas_call(prepare_kernel, out_shape=(jax.ShapeDtypeStruct((slabs, or...  1 us
    pallas_call x1, Pallas kernels, convolve(): pl.pallas_call(convolve_kernel, out_shape=jax.ShapeDtypeStruct(cells.shap...  0.97 us
  transfers between devices with their start and end apart: 1, of which 1 were waited for; matrix products, arithmetic and copies ran while one was open for 0% of the time, Pallas kernels for 2%

profile of v2, /device:TPU:0, one launch (start us, length us, event | category | flops | bytes accessed | tf_op | source)
XLA Modules:
  0.0 41.7 jit_solution(7310878470632254033)
XLA Ops:
  0.0 1.6 %copy.9 = f32[2,32,4,128]{3,2,0,1:T(4,128)} copy(f32[2,32,4,128]{3,2,1,0:T(4,128)} %bitcast.10) | data formatting | bytes 262144 | tf_op jit(solution)/shard_map/reshape;reshape | solution.py:297
  1.6 0.0 copy-start.6
  1.6 7.3 %all-to-all-start = ((f32[32,8,128]{2,1,0:T(8,128)}), f32[32,8,128]{2,1,0:T(8,128)S(1)}, u32[]{:S(2)}, u32[]{:S(2)}) async-start(f32[32,8,128]{2,1,0:T(8,128)} %bitcast.3), calls=%async_computation | async-start | bytes 262144 | tf_op jit(solution)/shard_map/all_to_all | solution.py:299
  8.9 0.0 copy-done.6
  8.9 0.1 copy.10.neighbors_ref
  9.0 0.0 copy-start.4
  9.0 0.7 %copy-done.4 = s32[256]{0:T(256)S(1)} copy-done((s32[256]{0:T(256)S(1)}, s32[256]{0:T(256)}, u32[]{:S(2)}) %copy-start.4) | copy-done | bytes 1048
  9.7 0.0 copy-start
  9.7 1.2 %copy-done = f32[2,8,16384]{2,1,0:T(8,128)S(1)} copy-done((f32[2,8,16384]{2,1,0:T(8,128)S(1)}, f32[2,8,16384]{2,1,0:T(8,128)}, u32[]{:S(2)}) %copy-start) | copy-done | bytes 1048600
  10.9 0.0 copy-start.1
  10.9 1.2 %copy-done.1 = f32[2,8,16384]{2,1,0:T(8,128)S(1)} copy-done((f32[2,8,16384]{2,1,0:T(8,128)S(1)}, f32[2,8,16384]{2,1,0:T(8,128)}, u32[]{:S(2)}) %copy-start.1) | copy-done | bytes 1048600
  12.2 1.0 %prepare.1 = (s32[2,128,128]{2,1,0:T(8,128)S(1)}, f32[2,2,8,8,128]{4,3,2,1,0:T(8,128)S(1)}) custom-call(s32[1]{0:T(128)} %bitcast.own_ref, s32[256,64]{1,0:T(8,128)S(1)} %copy.10.neighbors_ref, s32[2,128]{1,0:T(2,128)S(1)} %bitcast.9, f32[2,8,16384]{2,1,0:T(8,128)S(1)} %copy-done, f32[2,8,16384]{2,1,0:T(8,128)S(1)} %copy-done.1), custom_call_target="tpu_custom_call" | custom-call | tf_op jit(solution)/shard_map/prepare/pallas_call | solution.py:60
  13.2 0.0 copy-start.5
  13.2 3.9 %all-to-all-done.cells_ref = f32[32,8,128]{2,1,0:T(8,128)S(1)} async-done(((f32[32,8,128]{2,1,0:T(8,128)}), f32[32,8,128]{2,1,0:T(8,128)S(1)}, u32[]{:S(2)}, u32[]{:S(2)}) %all-to-all-start) | async-done | bytes 131104 | tf_op jit(solution)/shard_map/all_to_all | solution.py:299
  17.1 0.0 copy-done.5
  17.1 1.0 %convolve.1 = f32[32,8,128]{2,1,0:T(8,128)S(1)} custom-call(s32[8]{0:T(128)S(1)} %copy-done.5, f32[32,8,128]{2,1,0:T(8,128)S(1)} %all-to-all-done.cells_ref, f32[2,2,8,8,128]{4,3,2,1,0:T(8,128)S(1)} %get-tuple-element.7.coef_ref), custom_call_target="tpu_custom_call" | custom-call | tf_op jit(solution)/shard_map/convolve/pallas_call | solution.py:130
  18.1 0.0 copy-start.2
  18.1 0.0 copy-start.3
  18.1 10.5 %all_to_all.10.cells_ref = f32[32,8,128]{2,1,0:T(8,128)S(1)} all-to-all(f32[32,8,128]{2,1,0:T(8,128)S(1)} %convolve.1), channel_id=1, replica_groups=mesh['freq'=2,'atom'=16] {'freq','atom'}, dimensions={0} | all-to-all | bytes 262144 | tf_op jit(solution)/shard_map/all_to_all | solution.py:302
  28.7 0.0 copy-done.2
  28.7 0.0 copy-done.3
  28.7 13.0 %solve.1 = f32[2,2,128,128]{3,2,1,0:T(8,128)} custom-call(s32[1]{0:T(128)} %bitcast.own_ref, f32[32,8,128]{2,1,0:T(8,128)S(1)} %all_to_all.10.cells_ref, s32[2,128,128]{2,1,0:T(8,128)S(1)} %get-tuple-element.8.table_ref, f32[2,128,128]{2,1,0:T(8,128)S(1)} %copy-done.2, f32[1,128,128]{2,1,0:T(8,128)S(1)} %copy-done.3), custom_call_target="tpu_custom_call" | custom-call | tf_op jit(solution)/shard_map/solve/pallas_call | solution.py:271
Async XLA Ops:
  1.6 7.3 %copy-start.6 = (s32[256,64]{0,1:T(8,128)S(1)}, s32[256,64]{0,1:T(8,128)}, u32[]{:S(2)}) copy-start(s32[256,64]{0,1:T(8,128)} %param.10) | copy-start | bytes 196612
  1.6 15.5 %all-to-all-start = ((f32[32,8,128]{2,1,0:T(8,128)}), f32[32,8,128]{2,1,0:T(8,128)S(1)}, u32[]{:S(2)}, u32[]{:S(2)}) async-start(f32[32,8,128]{2,1,0:T(8,128)} %bitcast.3), calls=%async_computation | async-start | bytes 262144 | tf_op jit(solution)/shard_map/all_to_all | solution.py:299
  9.0 0.7 %copy-start.4 = (s32[256]{0:T(256)S(1)}, s32[256]{0:T(256)}, u32[]{:S(2)}) copy-start(s32[256]{0:T(256)} %param.11) | copy-start | bytes 3076
  9.7 1.2 %copy-start = (f32[2,8,16384]{2,1,0:T(8,128)S(1)}, f32[2,8,16384]{2,1,0:T(8,128)}, u32[]{:S(2)}) copy-start(f32[2,8,16384]{2,1,0:T(8,128)} %emit_ref.1) | copy-start | bytes 3145732
  10.9 1.2 %copy-start.1 = (f32[2,8,16384]{2,1,0:T(8,128)S(1)}, f32[2,8,16384]{2,1,0:T(8,128)}, u32[]{:S(2)}) copy-start(f32[2,8,16384]{2,1,0:T(8,128)} %absorb_ref.1) | copy-start | bytes 3145732
  13.2 4.0 %copy-start.5 = (s32[8]{0:T(128)S(1)}, s32[8]{0:T(128)}, u32[]{:S(2)}) copy-start(s32[8]{0:T(128)} %shifts_ref.1) | copy-start | bytes 100
  18.1 10.6 %copy-start.2 = (f32[2,128,128]{2,1,0:T(8,128)S(1)}, f32[2,128,128]{2,1,0:T(8,128)}, u32[]{:S(2)}) copy-start(f32[2,128,128]{2,1,0:T(8,128)} %diag_ref.1) | copy-start | bytes 393220
  18.1 10.6 %copy-start.3 = (f32[1,128,128]{2,1,0:T(8,128)S(1)}, f32[1,128,128]{2,1,0:T(8,128)}, u32[]{:S(2)}) copy-start(f32[1,128,128]{2,1,0:T(8,128)} %coup_ref.1) | copy-start | bytes 196612

commit v3 on v2

--- a/solution.py
+++ b/solution.py
@@ -16,7 +16,7 @@
 ENERGY_SPAN = 5.0
 
 LANES = 128
-RESIDUAL_LIMIT = 1e-4
+RESIDUAL_LIMIT = 1e-5
 
 AXES = ("freq", "atom")
 VMEM = pltpu.MemorySpace.VMEM
@@ -149,23 +149,13 @@
     )
 
 
-def full_dot(left, right):
-    return jnp.dot(left, right, precision=lax.Precision.HIGHEST, preferred_element_type=jnp.float32)
-
-
-def narrow_dot(left, right):
-    return jnp.dot(
-        left.astype(jnp.bfloat16), right.astype(jnp.bfloat16), preferred_element_type=jnp.float32
-    )
-
-
-def halves(pair):
-    order = pair.shape[1] // 2
-    return pair[:, :order], pair[:, order:]
-
-
-def pair_of(real, imag):
-    return jnp.concatenate([real, imag], axis=1)
+def pieces(value, count):
+    parts = []
+    for index in range(count):
+        parts.append(value.astype(jnp.bfloat16))
+        if index + 1 < count:
+            value = value - parts[-1].astype(jnp.float32)
+    return parts
 
 
 def unit_pair(order):
@@ -174,45 +164,103 @@
     return jnp.where(row == column, 1.0, 0.0).astype(jnp.float32)
 
 
-def start_of(matrix):
-    real, imag = halves(matrix)
-    scale = 1.0 / jnp.sum(matrix * matrix)
-    return pair_of(real.T * scale, imag.T * -scale)
-
-
-def invert(matrix, state_ref):
+def square_sum(pair):
+    squares = pair * pair
+    return jnp.sum(jnp.sum(squares, axis=0, keepdims=True), axis=1, keepdims=True)
+
+
+def adjoint(pair):
+    order = pair.shape[0]
+    return jnp.concatenate([pair[:, :order].T, -pair[:, order:].T], axis=1)
+
+
+class Multiplier:
+    def __init__(self, blocks):
+        self.blocks = blocks
+        self.turn = 0
+
+    def load(self, factor, transpose=False):
+        stage = self.turn
+        self.turn = 1 - stage
+        for unit in range(2):
+            pltpu.matmul_push_rhs(factor, stage, unit, transpose=transpose)
+        return stage
+
+    def feed(self, stage, *rows):
+        for block, left in rows:
+            half = left.shape[0] // 2
+            for unit in range(2):
+                pltpu.matmul_acc_lhs(
+                    self.blocks[block][unit],
+                    left[unit * half : (unit + 1) * half],
+                    load_staged_rhs=stage,
+                )
+            stage = None
+
+    def take(self, block):
+        return jnp.concatenate(
+            [pltpu.matmul_pop(self.blocks[block][unit]) for unit in range(2)], axis=0
+        )
+
+    def product(self, left, right, transpose=False):
+        for index, factor in enumerate(right):
+            stage = self.load(factor, transpose)
+            self.feed(stage, *[(0, piece) for piece in left[: len(left) - index]])
+        return self.take(0)
+
+
+def iterate(mxu, matrix, follow, count):
     order = matrix.shape[0]
-    start = start_of(matrix)
-    state_ref[:order] = start
-    state_ref[order:] = full_dot(matrix, embed(start))
-
-    def step(index, carry):
-        state = state_ref[...]
-        narrow = state.astype(jnp.bfloat16)
-        product = jnp.dot(narrow, embed(narrow[order:]), preferred_element_type=jnp.float32)
-        state_ref[...] = (state - product) + state
-        return carry
-
-    lax.fori_loop(0, INV_STEPS - EXACT_STEPS, step, 0)
-    current = state_ref[:order]
-    unit = unit_pair(order)
-    for _ in range(EXACT_STEPS):
-        residual = unit - full_dot(matrix, embed(current))
-        current = current + narrow_dot(current, embed(residual))
-    return current, jnp.sum(residual * residual)
-
-
-def invert_plain(matrix):
+    split = pieces(matrix, 2)
+    product = mxu.product(split, [embed(piece) for piece in split], transpose=True)
+    scale = 1.0 / square_sum(matrix)
+    x = adjoint(matrix) * scale
+    y = product * scale
+    for index in range(count):
+        narrow = y.astype(jnp.bfloat16)
+        stage = mxu.load(embed(narrow))
+        mxu.feed(stage, (0, narrow))
+        if index:
+            x = (x - mxu.take(1)) + x
+        mxu.feed(None, (1, x.astype(jnp.bfloat16)))
+        y = (y - mxu.take(0)) + y
+    x = (x - mxu.take(1)) + x
+
+    high, low = pieces(x, 2)
+    wide = mxu.load(embed(high))
+    rest = mxu.load(embed(low))
+    mxu.feed(wide, (0, split[0]), (0, split[1]))
+    mxu.feed(None, (1, follow[0]), (1, follow[1]))
+    mxu.feed(rest, (0, split[0]), (1, follow[0]))
+    residual = unit_pair(order) - mxu.take(0)
+    t = mxu.take(1)
+    r_high, r_low = pieces(residual, 2)
+    t_high, t_low = pieces(t, 2)
+    wide = mxu.load(embed(r_high))
+    rest = mxu.load(embed(r_low))
+    mxu.feed(wide, (0, r_high), (1, high), (1, low), (2, t_high), (2, t_low))
+    mxu.feed(rest, (1, high), (2, t_high))
+    residual = mxu.take(0)
+    stage = mxu.load(embed(residual.astype(jnp.bfloat16)))
+    x = x + mxu.take(1)
+    t = t + mxu.take(2)
+    mxu.feed(stage, (0, x.astype(jnp.bfloat16)), (1, t.astype(jnp.bfloat16)))
+    return x + mxu.take(0), t + mxu.take(1), square_sum(residual)
+
+
+def iterate_plain(mxu, matrix):
+    split = pieces(matrix, 3)
     unit = unit_pair(matrix.shape[0])
 
-    def step(index, current):
-        residue = 2.0 * unit - full_dot(matrix, embed(current))
-        return full_dot(current, embed(residue))
-
-    return lax.fori_loop(0, INV_STEPS, step, start_of(matrix))
-
-
-def solve_kernel(own_ref, cells_ref, table_ref, diag_ref, coup_ref, out_ref, matrix_ref, state_ref, *, energies):
+    def step(index, x):
+        right = [embed(piece) for piece in pieces(x, 3)]
+        residue = 2.0 * unit - mxu.product(split, right)
+        return mxu.product(pieces(x, 3), [embed(piece) for piece in pieces(residue, 3)])
+
+    return lax.fori_loop(0, INV_STEPS, step, adjoint(matrix) * (1.0 / square_sum(matrix)))
+
+
+def solve_kernel(own_ref, cells_ref, table_ref, diag_ref, coup_ref, out_ref, matrix_ref, *, energies):
     slabs, order, _ = diag_ref.shape
     unit = unit_pair(order)
     position = jnp.full((8, LANES), own_ref[0], jnp.int32).astype(jnp.float32)
@@ -238,31 +286,41 @@
                 matrix_ref[slab, rows, part * order : (part + 1) * order] = entry
 
     coup = coup_ref[0]
-    coup_t = coup.T
-
-    def right_by(pair, other):
-        real, imag = halves(pair)
-        return pair_of(full_dot(real, other), full_dot(imag, other))
-
-    def finish(invert_one):
-        last, last_norm = invert_one(matrix_ref[1])
-        left_of = full_dot(coup, last)
-        right_of = right_by(last, coup_t)
-        first, first_norm = invert_one(matrix_ref[0] - right_by(left_of, coup_t))
-        update = full_dot(full_dot(right_of, embed(first)), embed(left_of))
-        second = last + update
+    none = jnp.zeros_like(coup)
+    coup_left = jnp.concatenate([coup, none], axis=1)
+    coup_right = embed(jnp.concatenate([coup.T, none], axis=1))
+
+    def store(first, second):
         for part in range(2):
             columns = slice(part * order, (part + 1) * order)
             out_ref[part, 0] = first[:, columns]
             out_ref[part, 1] = second[:, columns]
-        return jnp.maximum(last_norm, first_norm), last_norm + first_norm
-
-    worst, total = finish(lambda matrix: invert(matrix, state_ref))
-    settled = jnp.logical_and(worst <= RESIDUAL_LIMIT, total == total)
-
-    @pl.when(jnp.logical_not(settled))
-    def _():
-        finish(lambda matrix: (invert_plain(matrix), jnp.float32(0.0)))
+
+    def body(*accumulators):
+        mxu = Multiplier([accumulators[2 * i : 2 * i + 2] for i in range(3)])
+        right = pieces(coup_right, 2)
+        last, left_of, last_norm = iterate(mxu, matrix_ref[1], pieces(coup_left, 2), INV_STEPS - EXACT_STEPS)
+        matrix = matrix_ref[0] - mxu.product(pieces(left_of, 2), right)
+        right_of = mxu.product(pieces(last, 2), right)
+        first, both, first_norm = iterate(mxu, matrix, pieces(right_of, 2), INV_STEPS - EXACT_STEPS)
+        update = mxu.product(pieces(both, 2), [embed(piece) for piece in pieces(left_of, 2)])
+        store(first, last + update)
+        worst = jnp.maximum(last_norm, first_norm)[0, 0]
+        settled = jnp.logical_and(worst <= RESIDUAL_LIMIT, last_norm[0, 0] + first_norm[0, 0] <= 2.0 * RESIDUAL_LIMIT)
+
+        @pl.when(jnp.logical_not(settled))
+        def _():
+            right = pieces(coup_right, 3)
+            last = iterate_plain(mxu, matrix_ref[1])
+            left_of = mxu.product(pieces(coup_left, 3), [embed(piece) for piece in pieces(last, 3)])
+            right_of = mxu.product(pieces(last, 3), right)
+            first = iterate_plain(mxu, matrix_ref[0] - mxu.product(pieces(left_of, 3), right))
+            both = mxu.product(pieces(right_of, 3), [embed(piece) for piece in pieces(first, 3)])
+            update = mxu.product(pieces(both, 3), [embed(piece) for piece in pieces(left_of, 3)])
+            store(first, last + update)
+
+    shape = (order // 2, 2 * order)
+    pl.run_scoped(body, *[pltpu.ACC(unit)(shape, jnp.float32) for _ in range(3) for unit in range(2)])
 
 
 def solve(own, cells, table, ham_diag, ham_coup, energies):
@@ -275,7 +333,6 @@
         out_specs=vmem,
         scratch_shapes=[
             pltpu.VMEM((slabs, order, 2 * order), jnp.float32),
-            pltpu.VMEM((2 * order, 2 * order), jnp.float32),
         ],
         compiler_params=pltpu.CompilerParams(vmem_limit_bytes=16 * 2**20),
         name="solve",

time: 42 us -> 39 us (0.929)
  Pallas kernels: 15 us -> 12 us
    pallas_call x1, Pallas kernels: 13 us -> 10 us  [solve(): pl.pallas_call(functools.partial(solve_kernel, energies=energies), out_sh...]
  transfers between devices with their start and end apart: 1 -> 1, of which waited for: 1 -> 1; matrix products, arithmetic and copies ran while one was open for 0% -> 0% of each run, Pallas kernels for 2% -> 3%
where the time goes in v3:
time: 39 us; the launch traced here: 38.7 us
  Pallas kernels  12 us (31%)
  blocking collectives  10.5 us (27%)
  starting transfers between devices  7.33 us (19%)
  local copies, waits for them, and re-layouts  4.82 us (12%)
  waiting for transfers between devices  3.94 us (10%)
    all_to_all x1, blocking collectives, on_device(): sigma = lax.all_to_all(sigma, AXES, 0, 0, tiled=True)  10.5 us
    pallas_call x1, Pallas kernels, solve(): pl.pallas_call(functools.partial(solve_kernel, energies=energies), out_sh...  10 us
    all_to_all x1, starting transfers between devices, on_device(): owned = lax.all_to_all(cells, AXES, 0, 0, tiled=True)  7.33 us
    all_to_all x1, waiting for transfers between devices, on_device(): owned = lax.all_to_all(cells, AXES, 0, 0, tiled=True)  3.94 us
    unnamed x15, local copies, waits for them, and re-layouts  3.24 us
    another operation x1, local copies, waits for them, and re-layouts, on_device(): cells = cells.reshape(2, devices, rows_per, LANES).transpose(1, 0, 2, 3)  1.58 us
    pallas_call x1, Pallas kernels, prepare(): pl.pallas_call(prepare_kernel, out_shape=(jax.ShapeDtypeStruct((slabs, or...  1 us
    pallas_call x1, Pallas kernels, convolve(): pl.pallas_call(convolve_kernel, out_shape=jax.ShapeDtypeStruct(cells.shap...  0.97 us
  transfers between devices with their start and end apart: 1, of which 1 were waited for; matrix products, arithmetic and copies ran while one was open for 0% of the time, Pallas kernels for 3%

profile of v3, /device:TPU:0, one launch (start us, length us, event | category | flops | bytes accessed | tf_op | source)
XLA Modules:
  0.0 38.7 jit_solution(4085226172640290231)
XLA Ops:
  0.0 1.6 %copy.9 = f32[2,32,4,128]{3,2,0,1:T(4,128)} copy(f32[2,32,4,128]{3,2,1,0:T(4,128)} %bitcast.10) | data formatting | bytes 262144 | tf_op jit(solution)/shard_map/reshape;reshape | solution.py:354
  1.6 0.0 copy-start.6
  1.6 7.3 %all-to-all-start = ((f32[32,8,128]{2,1,0:T(8,128)}), f32[32,8,128]{2,1,0:T(8,128)S(1)}, u32[]{:S(2)}, u32[]{:S(2)}) async-start(f32[32,8,128]{2,1,0:T(8,128)} %bitcast.3), calls=%async_computation | async-start | bytes 262144 | tf_op jit(solution)/shard_map/all_to_all | solution.py:356
  8.9 0.0 copy-done.6
  8.9 0.1 copy.10.neighbors_ref
  9.0 0.0 copy-start.4
  9.0 0.7 %copy-done.4 = s32[256]{0:T(256)S(1)} copy-done((s32[256]{0:T(256)S(1)}, s32[256]{0:T(256)}, u32[]{:S(2)}) %copy-start.4) | copy-done | bytes 1048
  9.7 0.0 copy-start
  9.7 1.2 %copy-done = f32[2,8,16384]{2,1,0:T(8,128)S(1)} copy-done((f32[2,8,16384]{2,1,0:T(8,128)S(1)}, f32[2,8,16384]{2,1,0:T(8,128)}, u32[]{:S(2)}) %copy-start) | copy-done | bytes 1048600
  10.9 0.0 copy-start.1
  10.9 1.2 %copy-done.1 = f32[2,8,16384]{2,1,0:T(8,128)S(1)} copy-done((f32[2,8,16384]{2,1,0:T(8,128)S(1)}, f32[2,8,16384]{2,1,0:T(8,128)}, u32[]{:S(2)}) %copy-start.1) | copy-done | bytes 1048600
  12.2 1.0 %prepare.1 = (s32[2,128,128]{2,1,0:T(8,128)S(1)}, f32[2,2,8,8,128]{4,3,2,1,0:T(8,128)S(1)}) custom-call(s32[1]{0:T(128)} %bitcast.own_ref, s32[256,64]{1,0:T(8,128)S(1)} %copy.10.neighbors_ref, s32[2,128]{1,0:T(2,128)S(1)} %bitcast.9, f32[2,8,16384]{2,1,0:T(8,128)S(1)} %copy-done, f32[2,8,16384]{2,1,0:T(8,128)S(1)} %copy-done.1), custom_call_target="tpu_custom_call" | custom-call | tf_op jit(solution)/shard_map/prepare/pallas_call | solution.py:60
  13.2 0.0 copy-start.5
  13.2 3.9 %all-to-all-done.cells_ref = f32[32,8,128]{2,1,0:T(8,128)S(1)} async-done(((f32[32,8,128]{2,1,0:T(8,128)}), f32[32,8,128]{2,1,0:T(8,128)S(1)}, u32[]{:S(2)}, u32[]{:S(2)}) %all-to-all-start) | async-done | bytes 131104 | tf_op jit(solution)/shard_map/all_to_all | solution.py:356
  17.1 0.0 copy-done.5
  17.1 1.0 %convolve.1 = f32[32,8,128]{2,1,0:T(8,128)S(1)} custom-call(s32[8]{0:T(128)S(1)} %copy-done.5, f32[32,8,128]{2,1,0:T(8,128)S(1)} %all-to-all-done.cells_ref, f32[2,2,8,8,128]{4,3,2,1,0:T(8,128)S(1)} %get-tuple-element.7.coef_ref), custom_call_target="tpu_custom_call" | custom-call | tf_op jit(solution)/shard_map/convolve/pallas_call | solution.py:130
  18.1 0.0 copy-start.2
  18.1 0.0 copy-start.3
  18.1 10.5 %all_to_all.10.cells_ref = f32[32,8,128]{2,1,0:T(8,128)S(1)} all-to-all(f32[32,8,128]{2,1,0:T(8,128)S(1)} %convolve.1), channel_id=1, replica_groups=mesh['freq'=2,'atom'=16] {'freq','atom'}, dimensions={0} | all-to-all | bytes 262144 | tf_op jit(solution)/shard_map/all_to_all | solution.py:359
  28.7 0.0 copy-done.2
  28.7 0.0 copy-done.3
  28.7 10.0 %solve.1 = f32[2,2,128,128]{3,2,1,0:T(8,128)} custom-call(s32[1]{0:T(128)} %bitcast.own_ref, f32[32,8,128]{2,1,0:T(8,128)S(1)} %all_to_all.10.cells_ref, s32[2,128,128]{2,1,0:T(8,128)S(1)} %get-tuple-element.8.table_ref, f32[2,128,128]{2,1,0:T(8,128)S(1)} %copy-done.2, f32[1,128,128]{2,1,0:T(8,128)S(1)} %copy-done.3), custom_call_target="tpu_custom_call" | custom-call | tf_op jit(solution)/shard_map/solve/pallas_call | solution.py:329
Async XLA Ops:
  1.6 7.3 %copy-start.6 = (s32[256,64]{0,1:T(8,128)S(1)}, s32[256,64]{0,1:T(8,128)}, u32[]{:S(2)}) copy-start(s32[256,64]{0,1:T(8,128)} %param.10) | copy-start | bytes 196612
  1.6 15.5 %all-to-all-start = ((f32[32,8,128]{2,1,0:T(8,128)}), f32[32,8,128]{2,1,0:T(8,128)S(1)}, u32[]{:S(2)}, u32[]{:S(2)}) async-start(f32[32,8,128]{2,1,0:T(8,128)} %bitcast.3), calls=%async_computation | async-start | bytes 262144 | tf_op jit(solution)/shard_map/all_to_all | solution.py:356
  9.0 0.7 %copy-start.4 = (s32[256]{0:T(256)S(1)}, s32[256]{0:T(256)}, u32[]{:S(2)}) copy-start(s32[256]{0:T(256)} %param.11) | copy-start | bytes 3076
  9.7 1.2 %copy-start = (f32[2,8,16384]{2,1,0:T(8,128)S(1)}, f32[2,8,16384]{2,1,0:T(8,128)}, u32[]{:S(2)}) copy-start(f32[2,8,16384]{2,1,0:T(8,128)} %emit_ref.1) | copy-start | bytes 3145732
  10.9 1.2 %copy-start.1 = (f32[2,8,16384]{2,1,0:T(8,128)S(1)}, f32[2,8,16384]{2,1,0:T(8,128)}, u32[]{:S(2)}) copy-start(f32[2,8,16384]{2,1,0:T(8,128)} %absorb_ref.1) | copy-start | bytes 3145732
  13.2 4.0 %copy-start.5 = (s32[8]{0:T(128)S(1)}, s32[8]{0:T(128)}, u32[]{:S(2)}) copy-start(s32[8]{0:T(128)} %shifts_ref.1) | copy-start | bytes 100
  18.1 10.6 %copy-start.2 = (f32[2,128,128]{2,1,0:T(8,128)S(1)}, f32[2,128,128]{2,1,0:T(8,128)}, u32[]{:S(2)}) copy-start(f32[2,128,128]{2,1,0:T(8,128)} %diag_ref.1) | copy-start | bytes 393220
  18.1 10.6 %copy-start.3 = (f32[1,128,128]{2,1,0:T(8,128)S(1)}, f32[1,128,128]{2,1,0:T(8,128)}, u32[]{:S(2)}) copy-start(f32[1,128,128]{2,1,0:T(8,128)} %coup_ref.1) | copy-start | bytes 196612

commit v4 on v3

--- a/solution.py
+++ b/solution.py
@@ -45,8 +45,8 @@
             imag = weights_ref[1, :, lanes]
             coef_ref[side, 0, :, row, :] = real
             coef_ref[side, 0, :, half + row, :] = real
-            coef_ref[side, 1, :, row, :] = -imag
-            coef_ref[side, 1, :, half + row, :] = imag
+            coef_ref[side, 1, :, row, :] = imag
+            coef_ref[side, 1, :, half + row, :] = -imag
 
 
 def prepare(own, neighbors, pair_count, emit_coup, absorb_coup, slabs, order, rows_per):
@@ -82,28 +82,26 @@
     )(own, neighbors, pair_count.reshape(slabs, order), emit_coup, absorb_coup)
 
 
-def convolve_kernel(shifts_ref, cells_ref, coef_ref, out_ref, plain_ref, swapped_ref):
+def convolve_kernel(shifts_hbm, cells_ref, coef_ref, out_ref, padded_ref, shifts_ref, sem):
     energies, height, _ = cells_ref.shape
     modes = coef_ref.shape[2]
+    half = height // 2
+    copy = pltpu.make_async_copy(shifts_hbm, shifts_ref, sem)
+    copy.start()
     edge = jnp.zeros((HALO, height, LANES), jnp.float32)
-    for ref in (plain_ref, swapped_ref):
-        ref[0:HALO] = edge
-        ref[HALO + energies : 2 * HALO + energies] = edge
-    group = 32 if energies % 32 == 0 else 1
+    padded_ref[0:HALO] = edge
+    padded_ref[HALO + energies : 2 * HALO + energies] = edge
+    group = 16 if energies % 16 == 0 else 1
 
     def load(index, carry):
-        for step in range(group):
-            energy = index * group + step
-            cell = cells_ref[energy]
-            plain_ref[HALO + energy] = cell
-            swapped_ref[HALO + energy] = jnp.concatenate(
-                [cell[height // 2 :], cell[: height // 2]], axis=0
-            )
+        rows = pl.ds(index * group, group)
+        padded_ref[pl.ds(HALO + index * group, group)] = cells_ref[rows]
         return carry
 
     def combine(index, carry):
         base = HALO + index * group
-        total = [jnp.zeros((height, LANES), jnp.float32)] * group
+        direct_sum = [jnp.zeros((height, LANES), jnp.float32)] * group
+        crossed_sum = list(direct_sum)
         for mode in range(modes):
             shift = shifts_ref[mode]
             for side in range(2):
@@ -111,32 +109,35 @@
                 direct = coef_ref[side, 0, mode]
                 crossed = coef_ref[side, 1, mode]
                 for step in range(group):
-                    total[step] = (
-                        total[step]
-                        + direct * plain_ref[first + step]
-                        + crossed * swapped_ref[first + step]
-                    )
+                    cell = padded_ref[first + step]
+                    direct_sum[step] = direct_sum[step] + direct * cell
+                    crossed_sum[step] = crossed_sum[step] + crossed * cell
         for step in range(group):
-            out_ref[index * group + step] = total[step]
+            turned = jnp.concatenate([crossed_sum[step][half:], crossed_sum[step][:half]], axis=0)
+            out_ref[index * group + step] = direct_sum[step] + turned
         return carry
 
-    lax.fori_loop(0, energies // group, load, 0)
-    lax.fori_loop(0, energies // group, combine, 0)
+    lax.fori_loop(0, energies // group, load, 0, unroll=energies // group <= 2)
+    copy.wait()
+    lax.fori_loop(0, energies // group, combine, 0, unroll=energies // group <= 2)
 
 
 def convolve(shifts, cells, coef):
     energies, height, _ = cells.shape
-    padded = pltpu.VMEM((energies + 2 * HALO, height, LANES), jnp.float32)
     return pl.pallas_call(
         convolve_kernel,
         out_shape=jax.ShapeDtypeStruct(cells.shape, jnp.float32),
         in_specs=[
-            pl.BlockSpec(memory_space=SMEM),
+            pl.BlockSpec(memory_space=pl.ANY),
             pl.BlockSpec(memory_space=VMEM),
             pl.BlockSpec(memory_space=VMEM),
         ],
         out_specs=pl.BlockSpec(memory_space=VMEM),
-        scratch_shapes=[padded, padded],
+        scratch_shapes=[
+            pltpu.VMEM((energies + 2 * HALO, height, LANES), jnp.float32),
+            pltpu.SMEM(shifts.shape, jnp.int32),
+            pltpu.SemaphoreType.DMA,
+        ],
         compiler_params=pltpu.CompilerParams(vmem_limit_bytes=16 * 2**20),
         name="convolve",
     )(shifts, cells, coef)
@@ -229,9 +230,8 @@
     high, low = pieces(x, 2)
     wide = mxu.load(embed(high))
     rest = mxu.load(embed(low))
-    mxu.feed(wide, (0, split[0]), (0, split[1]))
-    mxu.feed(None, (1, follow[0]), (1, follow[1]))
     mxu.feed(rest, (0, split[0]), (1, follow[0]))
+    mxu.feed(wide, (0, split[0]), (0, split[1]), (1, follow[0]), (1, follow[1]))
     residual = unit_pair(order) - mxu.take(0)
     t = mxu.take(1)
     r_high, r_low = pieces(residual, 2)
@@ -260,7 +260,11 @@
     return lax.fori_loop(0, INV_STEPS, step, adjoint(matrix) * (1.0 / square_sum(matrix)))
 
 
-def solve_kernel(own_ref, cells_ref, table_ref, diag_ref, coup_ref, out_ref, matrix_ref, *, energies):
+def pick(values, index, axis):
+    return jnp.take_along_axis(values, index, axis=axis, mode="promise_in_bounds")
+
+
+def solve_kernel(own_ref, cells_ref, table_ref, diag_ref, coup_ref, out_ref, matrix_ref, stage_ref, sems, *, energies):
     slabs, order, _ = diag_ref.shape
     unit = unit_pair(order)
     position = jnp.full((8, LANES), own_ref[0], jnp.int32).astype(jnp.float32)
@@ -268,7 +272,8 @@
     row = lax.broadcasted_iota(jnp.int32, (8, LANES), 0)
     lines = cells_ref.shape[1] // 2
     line_of = row // (8 // lines)
-    for slab in range(slabs):
+
+    def assemble(slab):
         for block in range(order // 8):
             cell = cells_ref[slab * (order // 8) + block]
             rows = slice(block * 8, block * 8 + 8)
@@ -276,8 +281,8 @@
             held = table >= 0
             lane = jnp.where(held, table, 0)
             for part in range(2):
-                spread = jnp.take_along_axis(cell, line_of + part * lines, axis=0)
-                sigma = jnp.where(held, jnp.take_along_axis(spread, lane, axis=1), 0.0)
+                spread = pick(cell, line_of + part * lines, 0)
+                sigma = jnp.where(held, pick(spread, lane, 1), 0.0)
                 eye = unit[rows, :order]
                 if part == 0:
                     entry = energy * eye - diag_ref[slab, rows, :] - sigma
@@ -285,28 +290,36 @@
                     entry = BROADEN * eye - sigma
                 matrix_ref[slab, rows, part * order : (part + 1) * order] = entry
 
+    assemble(1)
     coup = coup_ref[0]
     none = jnp.zeros_like(coup)
     coup_left = jnp.concatenate([coup, none], axis=1)
     coup_right = embed(jnp.concatenate([coup.T, none], axis=1))
 
-    def store(first, second):
+    def send(slab, pair):
         for part in range(2):
-            columns = slice(part * order, (part + 1) * order)
-            out_ref[part, 0] = first[:, columns]
-            out_ref[part, 1] = second[:, columns]
+            stage_ref[part, slab] = pair[:, part * order : (part + 1) * order]
+            pltpu.make_async_copy(stage_ref.at[part, slab], out_ref.at[part, slab], sems.at[part, slab]).start()
+
+    def sent():
+        for slab in range(slabs):
+            for part in range(2):
+                pltpu.make_async_copy(stage_ref.at[part, slab], out_ref.at[part, slab], sems.at[part, slab]).wait()
 
     def body(*accumulators):
         mxu = Multiplier([accumulators[2 * i : 2 * i + 2] for i in range(3)])
         right = pieces(coup_right, 2)
         last, left_of, last_norm = iterate(mxu, matrix_ref[1], pieces(coup_left, 2), INV_STEPS - EXACT_STEPS)
+        assemble(0)
         matrix = matrix_ref[0] - mxu.product(pieces(left_of, 2), right)
         right_of = mxu.product(pieces(last, 2), right)
         first, both, first_norm = iterate(mxu, matrix, pieces(right_of, 2), INV_STEPS - EXACT_STEPS)
+        send(0, first)
         update = mxu.product(pieces(both, 2), [embed(piece) for piece in pieces(left_of, 2)])
-        store(first, last + update)
+        send(1, last + update)
         worst = jnp.maximum(last_norm, first_norm)[0, 0]
         settled = jnp.logical_and(worst <= RESIDUAL_LIMIT, last_norm[0, 0] + first_norm[0, 0] <= 2.0 * RESIDUAL_LIMIT)
+        sent()
 
         @pl.when(jnp.logical_not(settled))
         def _():
@@ -317,7 +330,9 @@
             first = iterate_plain(mxu, matrix_ref[0] - mxu.product(pieces(left_of, 3), right))
             both = mxu.product(pieces(right_of, 3), [embed(piece) for piece in pieces(first, 3)])
             update = mxu.product(pieces(both, 3), [embed(piece) for piece in pieces(left_of, 3)])
-            store(first, last + update)
+            send(0, first)
+            send(1, last + update)
+            sent()
 
     shape = (order // 2, 2 * order)
     pl.run_scoped(body, *[pltpu.ACC(unit)(shape, jnp.float32) for _ in range(3) for unit in range(2)])
@@ -330,9 +345,11 @@
         functools.partial(solve_kernel, energies=energies),
         out_shape=jax.ShapeDtypeStruct((2, slabs, order, order), jnp.float32),
         in_specs=[pl.BlockSpec(memory_space=SMEM), vmem, vmem, vmem, vmem],
-        out_specs=vmem,
+        out_specs=pl.BlockSpec(memory_space=pl.ANY),
         scratch_shapes=[
             pltpu.VMEM((slabs, order, 2 * order), jnp.float32),
+            pltpu.VMEM((2, slabs, order, order), jnp.float32),
+            pltpu.SemaphoreType.DMA((2, slabs)),
         ],
         compiler_params=pltpu.CompilerParams(vmem_limit_bytes=16 * 2**20),
         name="solve",

time: 39 us -> 39 us (level)
  no operation moved by 1% of the time
where the time goes in v4:
time: 39 us; the launch traced here: 38.6 us
  Pallas kernels  11.9 us (31%)
  blocking collectives  10.5 us (27%)
  starting transfers between devices  7.33 us (19%)
  local copies, waits for them, and re-layouts  4.82 us (12%)
  waiting for transfers between devices  3.94 us (10%)
    all_to_all x1, blocking collectives, on_device(): sigma = lax.all_to_all(sigma, AXES, 0, 0, tiled=True)  10.5 us
    pallas_call x1, Pallas kernels, solve(): pl.pallas_call(functools.partial(solve_kernel, energies=energies), out_sh...  10.1 us
    all_to_all x1, starting transfers between devices, on_device(): owned = lax.all_to_all(cells, AXES, 0, 0, tiled=True)  7.33 us
    all_to_all x1, waiting for transfers between devices, on_device(): owned = lax.all_to_all(cells, AXES, 0, 0, tiled=True)  3.94 us
    unnamed x15, local copies, waits for them, and re-layouts  3.24 us
    another operation x1, local copies, waits for them, and re-layouts, on_device(): cells = cells.reshape(2, devices, rows_per, LANES).transpose(1, 0, 2, 3)  1.58 us
    pallas_call x1, Pallas kernels, prepare(): pl.pallas_call(prepare_kernel, out_shape=(jax.ShapeDtypeStruct((slabs, or...  0.99 us
    pallas_call x1, Pallas kernels, convolve(): pl.pallas_call(convolve_kernel, out_shape=jax.ShapeDtypeStruct(cells.shap...  0.87 us
  transfers between devices with their start and end apart: 1, of which 1 were waited for; matrix products, arithmetic and copies ran while one was open for 0% of the time, Pallas kernels for 3%

profile of v4, /device:TPU:0, one launch (start us, length us, event | category | flops | bytes accessed | tf_op | source)
XLA Modules:
  0.0 38.6 jit_solution(508608842040792265)
XLA Ops:
  0.0 1.6 %copy.9 = f32[2,32,4,128]{3,2,0,1:T(4,128)} copy(f32[2,32,4,128]{3,2,1,0:T(4,128)} %bitcast.10) | data formatting | bytes 262144 | tf_op jit(solution)/shard_map/reshape;reshape | solution.py:371
  1.6 0.0 copy-start.6
  1.6 7.3 %all-to-all-start = ((f32[32,8,128]{2,1,0:T(8,128)}), f32[32,8,128]{2,1,0:T(8,128)S(1)}, u32[]{:S(2)}, u32[]{:S(2)}) async-start(f32[32,8,128]{2,1,0:T(8,128)} %bitcast.3), calls=%async_computation | async-start | bytes 262144 | tf_op jit(solution)/shard_map/all_to_all | solution.py:373
  8.9 0.0 copy-done.6
  8.9 0.1 copy.10.neighbors_ref
  9.0 0.0 copy-start.4
  9.0 0.7 %copy-done.4 = s32[256]{0:T(256)S(1)} copy-done((s32[256]{0:T(256)S(1)}, s32[256]{0:T(256)}, u32[]{:S(2)}) %copy-start.4) | copy-done | bytes 1048
  9.7 0.0 copy-start
  9.7 1.2 %copy-done = f32[2,8,16384]{2,1,0:T(8,128)S(1)} copy-done((f32[2,8,16384]{2,1,0:T(8,128)S(1)}, f32[2,8,16384]{2,1,0:T(8,128)}, u32[]{:S(2)}) %copy-start) | copy-done | bytes 1048600
  10.9 0.0 copy-start.1
  10.9 1.2 %copy-done.1 = f32[2,8,16384]{2,1,0:T(8,128)S(1)} copy-done((f32[2,8,16384]{2,1,0:T(8,128)S(1)}, f32[2,8,16384]{2,1,0:T(8,128)}, u32[]{:S(2)}) %copy-start.1) | copy-done | bytes 1048600
  12.2 1.0 %prepare.1 = (s32[2,128,128]{2,1,0:T(8,128)S(1)}, f32[2,2,8,8,128]{4,3,2,1,0:T(8,128)S(1)}) custom-call(s32[1]{0:T(128)} %bitcast.own_ref, s32[256,64]{1,0:T(8,128)S(1)} %copy.10.neighbors_ref, s32[2,128]{1,0:T(2,128)S(1)} %bitcast.9, f32[2,8,16384]{2,1,0:T(8,128)S(1)} %copy-done, f32[2,8,16384]{2,1,0:T(8,128)S(1)} %copy-done.1), custom_call_target="tpu_custom_call" | custom-call | tf_op jit(solution)/shard_map/prepare/pallas_call | solution.py:60
  13.2 0.0 copy-start.5
  13.2 3.9 %all-to-all-done.cells_ref = f32[32,8,128]{2,1,0:T(8,128)S(1)} async-done(((f32[32,8,128]{2,1,0:T(8,128)}), f32[32,8,128]{2,1,0:T(8,128)S(1)}, u32[]{:S(2)}, u32[]{:S(2)}) %all-to-all-start) | async-done | bytes 131104 | tf_op jit(solution)/shard_map/all_to_all | solution.py:373
  17.1 0.0 copy-done.5
  17.1 0.9 %convolve.1 = f32[32,8,128]{2,1,0:T(8,128)S(1)} custom-call(s32[8]{0:T(128)S(1)} %copy-done.5, f32[32,8,128]{2,1,0:T(8,128)S(1)} %all-to-all-done.cells_ref, f32[2,2,8,8,128]{4,3,2,1,0:T(8,128)S(1)} %get-tuple-element.7.coef_ref), custom_call_target="tpu_custom_call" | custom-call | tf_op jit(solution)/shard_map/convolve/pallas_call | solution.py:127
  18.0 0.0 copy-start.2
  18.0 0.0 copy-start.3
  18.0 10.5 %all_to_all.10.cells_ref = f32[32,8,128]{2,1,0:T(8,128)S(1)} all-to-all(f32[32,8,128]{2,1,0:T(8,128)S(1)} %convolve.1), channel_id=1, replica_groups=mesh['freq'=2,'atom'=16] {'freq','atom'}, dimensions={0} | all-to-all | bytes 262144 | tf_op jit(solution)/shard_map/all_to_all | solution.py:376
  28.6 0.0 copy-done.2
  28.6 0.0 copy-done.3
  28.6 10.1 %solve.1 = f32[2,2,128,128]{3,2,1,0:T(8,128)} custom-call(s32[1]{0:T(128)} %bitcast.own_ref, f32[32,8,128]{2,1,0:T(8,128)S(1)} %all_to_all.10.cells_ref, s32[2,128,128]{2,1,0:T(8,128)S(1)} %get-tuple-element.8.table_ref, f32[2,128,128]{2,1,0:T(8,128)S(1)} %copy-done.2, f32[1,128,128]{2,1,0:T(8,128)S(1)} %copy-done.3), custom_call_target="tpu_custom_call" | custom-call | tf_op jit(solution)/shard_map/solve/pallas_call | solution.py:344
Async XLA Ops:
  1.6 7.3 %copy-start.6 = (s32[256,64]{0,1:T(8,128)S(1)}, s32[256,64]{0,1:T(8,128)}, u32[]{:S(2)}) copy-start(s32[256,64]{0,1:T(8,128)} %param.10) | copy-start | bytes 196612
  1.6 15.5 %all-to-all-start = ((f32[32,8,128]{2,1,0:T(8,128)}), f32[32,8,128]{2,1,0:T(8,128)S(1)}, u32[]{:S(2)}, u32[]{:S(2)}) async-start(f32[32,8,128]{2,1,0:T(8,128)} %bitcast.3), calls=%async_computation | async-start | bytes 262144 | tf_op jit(solution)/shard_map/all_to_all | solution.py:373
  9.0 0.7 %copy-start.4 = (s32[256]{0:T(256)S(1)}, s32[256]{0:T(256)}, u32[]{:S(2)}) copy-start(s32[256]{0:T(256)} %param.11) | copy-start | bytes 3076
  9.7 1.2 %copy-start = (f32[2,8,16384]{2,1,0:T(8,128)S(1)}, f32[2,8,16384]{2,1,0:T(8,128)}, u32[]{:S(2)}) copy-start(f32[2,8,16384]{2,1,0:T(8,128)} %emit_ref.1) | copy-start | bytes 3145732
  10.9 1.2 %copy-start.1 = (f32[2,8,16384]{2,1,0:T(8,128)S(1)}, f32[2,8,16384]{2,1,0:T(8,128)}, u32[]{:S(2)}) copy-start(f32[2,8,16384]{2,1,0:T(8,128)} %absorb_ref.1) | copy-start | bytes 3145732
  13.2 4.0 %copy-start.5 = (s32[8]{0:T(128)S(1)}, s32[8]{0:T(128)}, u32[]{:S(2)}) copy-start(s32[8]{0:T(128)} %shifts_hbm.1) | copy-start | bytes 100
  18.0 10.6 %copy-start.2 = (f32[2,128,128]{2,1,0:T(8,128)S(1)}, f32[2,128,128]{2,1,0:T(8,128)}, u32[]{:S(2)}) copy-start(f32[2,128,128]{2,1,0:T(8,128)} %diag_ref.1) | copy-start | bytes 393220
  18.0 10.6 %copy-start.3 = (f32[1,128,128]{2,1,0:T(8,128)S(1)}, f32[1,128,128]{2,1,0:T(8,128)}, u32[]{:S(2)}) copy-start(f32[1,128,128]{2,1,0:T(8,128)} %coup_ref.1) | copy-start | bytes 196612

commit v5 on v4

--- a/solution.py
+++ b/solution.py
@@ -16,33 +16,50 @@
 ENERGY_SPAN = 5.0
 
 LANES = 128
-RESIDUAL_LIMIT = 1e-5
+RESIDUAL_LIMIT = 2e-5
 
 AXES = ("freq", "atom")
 VMEM = pltpu.MemorySpace.VMEM
 SMEM = pltpu.MemorySpace.SMEM
 
 
-def prepare_kernel(own_ref, neighbors_ref, count_ref, emit_ref, absorb_ref, table_ref, coef_ref):
+def prepare_kernel(
+    own_ref, neighbors_hbm, count_hbm, emit_hbm, absorb_hbm, table_ref, coef_ref, neighbors_ref, count_ref, weights_ref, sems
+):
     slabs, order, _ = table_ref.shape
-    slots = neighbors_ref.shape[1]
+    slots = neighbors_ref.shape[0]
     half = coef_ref.shape[3] // 2
+    width = half * LANES
+    block = jnp.minimum(own_ref[0], emit_hbm.shape[2] // width - 1)
+    lanes = pl.ds(pl.multiple_of(block * width, LANES), width)
+    copies = [
+        pltpu.make_async_copy(neighbors_hbm, neighbors_ref, sems.at[0]),
+        pltpu.make_async_copy(count_hbm, count_ref, sems.at[1]),
+        pltpu.make_async_copy(emit_hbm.at[:, :, lanes], weights_ref.at[0], sems.at[2]),
+        pltpu.make_async_copy(absorb_hbm.at[:, :, lanes], weights_ref.at[1], sems.at[3]),
+    ]
+    for copy in copies:
+        copy.start()
+    copies[0].wait()
+    copies[1].wait()
     slot_id = lax.broadcasted_iota(jnp.int32, (slots, order), 0)
     column = lax.broadcasted_iota(jnp.int32, (order, order), 0)
     lane = lax.broadcasted_iota(jnp.int32, (order, order), 1)
     offset = lax.rem(lane, LANES // slots) * slots
     for slab in range(slabs):
-        listed = neighbors_ref[slab * order : (slab + 1) * order, :].T
+        listed = neighbors_ref[:, slab * order : (slab + 1) * order]
         listed = jnp.where(slot_id < count_ref[slab : slab + 1, :], listed, -1)
         found = jnp.full((order, order), -1, jnp.int32)
         for slot in range(slots):
             found = jnp.where(listed[slot : slot + 1, :] == column, slot, found)
         table_ref[slab] = jnp.where(found >= 0, found + offset, -1).T
-    for side, weights_ref in enumerate((emit_ref, absorb_ref)):
+    copies[2].wait()
+    copies[3].wait()
+    for side in range(2):
         for row in range(half):
-            lanes = slice(row * LANES, (row + 1) * LANES)
-            real = weights_ref[0, :, lanes]
-            imag = weights_ref[1, :, lanes]
+            part = slice(row * LANES, (row + 1) * LANES)
+            real = weights_ref[side, 0, :, part]
+            imag = weights_ref[side, 1, :, part]
             coef_ref[side, 0, :, row, :] = real
             coef_ref[side, 0, :, half + row, :] = real
             coef_ref[side, 1, :, row, :] = imag
@@ -51,11 +68,8 @@
 
 def prepare(own, neighbors, pair_count, emit_coup, absorb_coup, slabs, order, rows_per):
     modes = emit_coup.shape[1]
-    blocks = emit_coup.shape[2] // (rows_per * LANES)
-    weights = pl.BlockSpec(
-        (2, modes, rows_per * LANES),
-        lambda i, own_ref: (0, 0, jnp.minimum(own_ref[0], blocks - 1)),
-    )
+    atoms, slots = neighbors.shape
+    arrays = (neighbors.T, pair_count.reshape(slabs, order), emit_coup, absorb_coup)
     whole = lambda *shape: pl.BlockSpec(shape, lambda i, own_ref: (0,) * len(shape))
     return pl.pallas_call(
         prepare_kernel,
@@ -66,20 +80,21 @@
         grid_spec=pltpu.PrefetchScalarGridSpec(
             num_scalar_prefetch=1,
             grid=(1,),
-            in_specs=[
-                whole(*neighbors.shape),
-                whole(slabs, order),
-                weights,
-                weights,
-            ],
+            in_specs=[pl.BlockSpec(memory_space=pltpu.HBM)] * 4,
             out_specs=(
                 whole(slabs, order, order),
                 whole(2, 2, modes, 2 * rows_per, LANES),
             ),
+            scratch_shapes=[
+                pltpu.VMEM((slots, atoms), jnp.int32),
+                pltpu.VMEM((slabs, order), jnp.int32),
+                pltpu.VMEM((2, 2, modes, rows_per * LANES), jnp.float32),
+                pltpu.SemaphoreType.DMA((4,)),
+            ],
         ),
         compiler_params=pltpu.CompilerParams(vmem_limit_bytes=16 * 2**20),
         name="prepare",
-    )(own, neighbors, pair_count.reshape(slabs, order), emit_coup, absorb_coup)
+    )(own, *[pltpu.with_memory_space_constraint(array, pltpu.HBM) for array in arrays])
 
 
 def convolve_kernel(shifts_hbm, cells_ref, coef_ref, out_ref, padded_ref, shifts_ref, sem):
@@ -213,7 +228,7 @@
 def iterate(mxu, matrix, follow, count):
     order = matrix.shape[0]
     split = pieces(matrix, 2)
-    product = mxu.product(split, [embed(piece) for piece in split], transpose=True)
+    product = mxu.product(split[:1], [embed(split[0])], transpose=True)
     scale = 1.0 / square_sum(matrix)
     x = adjoint(matrix) * scale
     y = product * scale
@@ -238,14 +253,15 @@
     t_high, t_low = pieces(t, 2)
     wide = mxu.load(embed(r_high))
     rest = mxu.load(embed(r_low))
-    mxu.feed(wide, (0, r_high), (1, high), (1, low), (2, t_high), (2, t_low))
-    mxu.feed(rest, (1, high), (2, t_high))
+    mxu.feed(wide, (0, r_high), (2, t_high), (2, t_low), (1, high), (1, low))
+    mxu.feed(rest, (2, t_high), (1, high))
     residual = mxu.take(0)
     stage = mxu.load(embed(residual.astype(jnp.bfloat16)))
+    t = t + mxu.take(2)
     x = x + mxu.take(1)
-    t = t + mxu.take(2)
-    mxu.feed(stage, (0, x.astype(jnp.bfloat16)), (1, t.astype(jnp.bfloat16)))
-    return x + mxu.take(0), t + mxu.take(1), square_sum(residual)
+    mxu.feed(stage, (1, t.astype(jnp.bfloat16)), (0, x.astype(jnp.bfloat16)))
+    t = t + mxu.take(1)
+    return x + mxu.take(0), t, square_sum(residual)
 
 
 def iterate_plain(mxu, matrix):

time: 39 us -> 38.3 us (0.982)
  local copies, waits for them, and re-layouts: 4.82 us -> 1.6 us
  waiting for transfers between devices: 3.94 us -> 6.34 us
  Pallas kernels: 11.9 us -> 12.6 us
  blocking collectives: 10.5 us -> 10 us
    unnamed x15 -> x6, local copies, waits for them, and re-layouts: 3.24 us -> 0.02 us
    all_to_all x1, waiting for transfers between devices: 3.94 us -> 6.34 us  [on_device(): owned = lax.all_to_all(cells, AXES, 0, 0, tiled=True)]
    pallas_call x1, Pallas kernels: 0.99 us -> 1.83 us  [prepare(): pl.pallas_call(prepare_kernel, out_shape=(jax.ShapeDtypeStruct((slabs, or...]
    all_to_all x1, blocking collectives: 10.5 us -> 10 us  [on_device(): sigma = lax.all_to_all(sigma, AXES, 0, 0, tiled=True)]
  transfers between devices with their start and end apart: 1 -> 1, of which waited for: 1 -> 1; matrix products, arithmetic and copies ran while one was open for 0% -> 0% of each run, Pallas kernels for 3% -> 5%
where the time goes in v5:
time: 38.3 us; the launch traced here: 38 us
  Pallas kernels  12.6 us (33%)
  blocking collectives  10 us (26%)
  starting transfers between devices  7.33 us (19%)
  waiting for transfers between devices  6.34 us (17%)
  local copies, waits for them, and re-layouts  1.6 us (4%)
    all_to_all x1, blocking collectives, on_device(): sigma = lax.all_to_all(sigma, AXES, 0, 0, tiled=True)  10 us
    pallas_call x1, Pallas kernels, solve(): pl.pallas_call(functools.partial(solve_kernel, energies=energies), out_sh...  9.93 us
    all_to_all x1, starting transfers between devices, on_device(): owned = lax.all_to_all(cells, AXES, 0, 0, tiled=True)  7.33 us
    all_to_all x1, waiting for transfers between devices, on_device(): owned = lax.all_to_all(cells, AXES, 0, 0, tiled=True)  6.34 us
    pallas_call x1, Pallas kernels, prepare(): pl.pallas_call(prepare_kernel, out_shape=(jax.ShapeDtypeStruct((slabs, or...  1.83 us
    another operation x1, local copies, waits for them, and re-layouts, on_device(): cells = cells.reshape(2, devices, rows_per, LANES).transpose(1, 0, 2, 3)  1.58 us
    pallas_call x1, Pallas kernels, convolve(): pl.pallas_call(convolve_kernel, out_shape=jax.ShapeDtypeStruct(cells.shap...  0.87 us
  transfers between devices with their start and end apart: 1, of which 1 were waited for; matrix products, arithmetic and copies ran while one was open for 0% of the time, Pallas kernels for 5%

profile of v5, /device:TPU:0, one launch (start us, length us, event | category | flops | bytes accessed | tf_op | source)
XLA Modules:
  0.0 38.0 jit_solution(4909644136207362040)
XLA Ops:
  0.0 1.6 %copy.9 = f32[2,32,4,128]{3,2,0,1:T(4,128)} copy(f32[2,32,4,128]{3,2,1,0:T(4,128)} %bitcast.10) | data formatting | bytes 262144 | tf_op jit(solution)/shard_map/reshape;reshape | solution.py:387
  1.6 7.3 %all-to-all-start = ((f32[32,8,128]{2,1,0:T(8,128)}), f32[32,8,128]{2,1,0:T(8,128)S(1)}, u32[]{:S(2)}, u32[]{:S(2)}) async-start(f32[32,8,128]{2,1,0:T(8,128)} %bitcast.3), calls=%async_computation | async-start | bytes 262144 | tf_op jit(solution)/shard_map/all_to_all | solution.py:389
  8.9 1.8 %prepare.1 = (s32[2,128,128]{2,1,0:T(8,128)S(1)}, f32[2,2,8,8,128]{4,3,2,1,0:T(8,128)S(1)}) custom-call(s32[1]{0:T(128)} %bitcast.own_ref, s32[64,256]{1,0:T(8,128)} %bitcast.11, s32[2,128]{1,0:T(2,128)} %bitcast.12, f32[2,8,16384]{2,1,0:T(8,128)} %emit_hbm.1, f32[2,8,16384]{2,1,0:T(8,128)} %absorb_hbm.1), custom_call_target="tpu_custom_call" | custom-call | tf_op jit(solution)/shard_map/prepare/pallas_call | solution.py:74
  10.8 0.0 copy-start.2
  10.8 6.3 %all-to-all-done.cells_ref = f32[32,8,128]{2,1,0:T(8,128)S(1)} async-done(((f32[32,8,128]{2,1,0:T(8,128)}), f32[32,8,128]{2,1,0:T(8,128)S(1)}, u32[]{:S(2)}, u32[]{:S(2)}) %all-to-all-start) | async-done | bytes 131104 | tf_op jit(solution)/shard_map/all_to_all | solution.py:389
  17.1 0.0 copy-done.2
  17.1 0.9 %convolve.1 = f32[32,8,128]{2,1,0:T(8,128)S(1)} custom-call(s32[8]{0:T(128)S(1)} %copy-done.2, f32[32,8,128]{2,1,0:T(8,128)S(1)} %all-to-all-done.cells_ref, f32[2,2,8,8,128]{4,3,2,1,0:T(8,128)S(1)} %get-tuple-element.7.coef_ref), custom_call_target="tpu_custom_call" | custom-call | tf_op jit(solution)/shard_map/convolve/pallas_call | solution.py:142
  18.0 0.0 copy-start
  18.0 0.0 copy-start.1
  18.0 10.0 %all_to_all.10.cells_ref = f32[32,8,128]{2,1,0:T(8,128)S(1)} all-to-all(f32[32,8,128]{2,1,0:T(8,128)S(1)} %convolve.1), channel_id=1, replica_groups=mesh['freq'=2,'atom'=16] {'freq','atom'}, dimensions={0} | all-to-all | bytes 262144 | tf_op jit(solution)/shard_map/all_to_all | solution.py:392
  28.1 0.0 copy-done
  28.1 0.0 copy-done.1
  28.1 9.9 %solve.1 = f32[2,2,128,128]{3,2,1,0:T(8,128)} custom-call(s32[1]{0:T(128)} %bitcast.own_ref, f32[32,8,128]{2,1,0:T(8,128)S(1)} %all_to_all.10.cells_ref, s32[2,128,128]{2,1,0:T(8,128)S(1)} %get-tuple-element.8.table_ref, f32[2,128,128]{2,1,0:T(8,128)S(1)} %copy-done, f32[1,128,128]{2,1,0:T(8,128)S(1)} %copy-done.1), custom_call_target="tpu_custom_call" | custom-call | tf_op jit(solution)/shard_map/solve/pallas_call | solution.py:360
Async XLA Ops:
  1.6 15.5 %all-to-all-start = ((f32[32,8,128]{2,1,0:T(8,128)}), f32[32,8,128]{2,1,0:T(8,128)S(1)}, u32[]{:S(2)}, u32[]{:S(2)}) async-start(f32[32,8,128]{2,1,0:T(8,128)} %bitcast.3), calls=%async_computation | async-start | bytes 262144 | tf_op jit(solution)/shard_map/all_to_all | solution.py:389
  10.8 6.4 %copy-start.2 = (s32[8]{0:T(128)S(1)}, s32[8]{0:T(128)}, u32[]{:S(2)}) copy-start(s32[8]{0:T(128)} %shifts_hbm.1) | copy-start | bytes 100
  18.0 10.1 %copy-start = (f32[2,128,128]{2,1,0:T(8,128)S(1)}, f32[2,128,128]{2,1,0:T(8,128)}, u32[]{:S(2)}) copy-start(f32[2,128,128]{2,1,0:T(8,128)} %diag_ref.1) | copy-start | bytes 393220
  18.0 10.1 %copy-start.1 = (f32[1,128,128]{2,1,0:T(8,128)S(1)}, f32[1,128,128]{2,1,0:T(8,128)}, u32[]{:S(2)}) copy-start(f32[1,128,128]{2,1,0:T(8,128)} %coup_ref.1) | copy-start | bytes 196612

commit v6 on v5

--- a/solution.py
+++ b/solution.py
@@ -24,7 +24,23 @@
 
 
 def prepare_kernel(
-    own_ref, neighbors_hbm, count_hbm, emit_hbm, absorb_hbm, table_ref, coef_ref, neighbors_ref, count_ref, weights_ref, sems
+    own_ref,
+    neighbors_hbm,
+    count_hbm,
+    shifts_hbm,
+    emit_hbm,
+    absorb_hbm,
+    table_ref,
+    coef_ref,
+    steps_ref,
+    energy_ref,
+    neighbors_ref,
+    count_ref,
+    shifts_ref,
+    weights_ref,
+    sems,
+    *,
+    energies,
 ):
     slabs, order, _ = table_ref.shape
     slots = neighbors_ref.shape[0]
@@ -37,9 +53,12 @@
         pltpu.make_async_copy(count_hbm, count_ref, sems.at[1]),
         pltpu.make_async_copy(emit_hbm.at[:, :, lanes], weights_ref.at[0], sems.at[2]),
         pltpu.make_async_copy(absorb_hbm.at[:, :, lanes], weights_ref.at[1], sems.at[3]),
+        pltpu.make_async_copy(shifts_hbm, shifts_ref, sems.at[4]),
     ]
     for copy in copies:
         copy.start()
+    position = jnp.full(energy_ref.shape, own_ref[0], jnp.int32).astype(jnp.float32)
+    energy_ref[...] = ENERGY_LOW + ENERGY_SPAN * position / energies
     copies[0].wait()
     copies[1].wait()
     slot_id = lax.broadcasted_iota(jnp.int32, (slots, order), 0)
@@ -53,8 +72,10 @@
         for slot in range(slots):
             found = jnp.where(listed[slot : slot + 1, :] == column, slot, found)
         table_ref[slab] = jnp.where(found >= 0, found + offset, -1).T
-    copies[2].wait()
-    copies[3].wait()
+    for copy in copies[2:]:
+        copy.wait()
+    for mode in range(steps_ref.shape[0]):
+        steps_ref[mode] = jnp.full(steps_ref.shape[1:], shifts_ref[mode], jnp.int32)
     for side in range(2):
         for row in range(half):
             part = slice(row * LANES, (row + 1) * LANES)
@@ -66,30 +87,35 @@
             coef_ref[side, 1, :, half + row, :] = -imag
 
 
-def prepare(own, neighbors, pair_count, emit_coup, absorb_coup, slabs, order, rows_per):
+def prepare(own, neighbors, pair_count, shifts, emit_coup, absorb_coup, slabs, order, rows_per, energies):
     modes = emit_coup.shape[1]
     atoms, slots = neighbors.shape
-    arrays = (neighbors.T, pair_count.reshape(slabs, order), emit_coup, absorb_coup)
+    arrays = (neighbors.T, pair_count.reshape(slabs, order), shifts, emit_coup, absorb_coup)
     whole = lambda *shape: pl.BlockSpec(shape, lambda i, own_ref: (0,) * len(shape))
     return pl.pallas_call(
-        prepare_kernel,
+        functools.partial(prepare_kernel, energies=energies),
         out_shape=(
             jax.ShapeDtypeStruct((slabs, order, order), jnp.int32),
             jax.ShapeDtypeStruct((2, 2, modes, 2 * rows_per, LANES), jnp.float32),
+            jax.ShapeDtypeStruct((modes, 8, LANES), jnp.int32),
+            jax.ShapeDtypeStruct((8, LANES), jnp.float32),
         ),
         grid_spec=pltpu.PrefetchScalarGridSpec(
             num_scalar_prefetch=1,
             grid=(1,),
-            in_specs=[pl.BlockSpec(memory_space=pltpu.HBM)] * 4,
+            in_specs=[pl.BlockSpec(memory_space=pltpu.HBM)] * 5,
             out_specs=(
                 whole(slabs, order, order),
                 whole(2, 2, modes, 2 * rows_per, LANES),
+                whole(modes, 8, LANES),
+                whole(8, LANES),
             ),
             scratch_shapes=[
                 pltpu.VMEM((slots, atoms), jnp.int32),
                 pltpu.VMEM((slabs, order), jnp.int32),
+                pltpu.SMEM((modes,), jnp.int32),
                 pltpu.VMEM((2, 2, modes, rows_per * LANES), jnp.float32),
-                pltpu.SemaphoreType.DMA((4,)),
+                pltpu.SemaphoreType.DMA((5,)),
             ],
         ),
         compiler_params=pltpu.CompilerParams(vmem_limit_bytes=16 * 2**20),
@@ -97,12 +123,11 @@
     )(own, *[pltpu.with_memory_space_constraint(array, pltpu.HBM) for array in arrays])
 
 
-def convolve_kernel(shifts_hbm, cells_ref, coef_ref, out_ref, padded_ref, shifts_ref, sem):
+def convolve_kernel(steps_ref, cells_ref, coef_ref, out_ref, padded_ref):
     energies, height, _ = cells_ref.shape
     modes = coef_ref.shape[2]
     half = height // 2
-    copy = pltpu.make_async_copy(shifts_hbm, shifts_ref, sem)
-    copy.start()
+    shifts = [steps_ref[mode][0, 0] for mode in range(modes)]
     edge = jnp.zeros((HALO, height, LANES), jnp.float32)
     padded_ref[0:HALO] = edge
     padded_ref[HALO + energies : 2 * HALO + energies] = edge
@@ -118,7 +143,7 @@
         direct_sum = [jnp.zeros((height, LANES), jnp.float32)] * group
         crossed_sum = list(direct_sum)
         for mode in range(modes):
-            shift = shifts_ref[mode]
+            shift = shifts[mode]
             for side in range(2):
                 first = base + (shift if side else -shift)
                 direct = coef_ref[side, 0, mode]
@@ -133,29 +158,21 @@
         return carry
 
     lax.fori_loop(0, energies // group, load, 0, unroll=energies // group <= 2)
-    copy.wait()
     lax.fori_loop(0, energies // group, combine, 0, unroll=energies // group <= 2)
 
 
-def convolve(shifts, cells, coef):
+def convolve(steps, cells, coef):
     energies, height, _ = cells.shape
+    vmem = pl.BlockSpec(memory_space=VMEM)
     return pl.pallas_call(
         convolve_kernel,
         out_shape=jax.ShapeDtypeStruct(cells.shape, jnp.float32),
-        in_specs=[
-            pl.BlockSpec(memory_space=pl.ANY),
-            pl.BlockSpec(memory_space=VMEM),
-            pl.BlockSpec(memory_space=VMEM),
-        ],
-        out_specs=pl.BlockSpec(memory_space=VMEM),
-        scratch_shapes=[
-            pltpu.VMEM((energies + 2 * HALO, height, LANES), jnp.float32),
-            pltpu.SMEM(shifts.shape, jnp.int32),
-            pltpu.SemaphoreType.DMA,
-        ],
+        in_specs=[vmem, vmem, vmem],
+        out_specs=vmem,
+        scratch_shapes=[pltpu.VMEM((energies + 2 * HALO, height, LANES), jnp.float32)],
         compiler_params=pltpu.CompilerParams(vmem_limit_bytes=16 * 2**20),
         name="convolve",
-    )(shifts, cells, coef)
+    )(steps, cells, coef)
 
 
 def embed(pair):
@@ -280,11 +297,10 @@
     return jnp.take_along_axis(values, index, axis=axis, mode="promise_in_bounds")
 
 
-def solve_kernel(own_ref, cells_ref, table_ref, diag_ref, coup_ref, out_ref, matrix_ref, stage_ref, sems, *, energies):
+def solve_kernel(energy_ref, cells_ref, table_ref, diag_ref, coup_ref, out_ref, matrix_ref, stage_ref, sems):
     slabs, order, _ = diag_ref.shape
     unit = unit_pair(order)
-    position = jnp.full((8, LANES), own_ref[0], jnp.int32).astype(jnp.float32)
-    energy = (ENERGY_LOW + ENERGY_SPAN * position / energies)[0:1, 0:1]
+    energy = energy_ref[...]
     row = lax.broadcasted_iota(jnp.int32, (8, LANES), 0)
     lines = cells_ref.shape[1] // 2
     line_of = row // (8 // lines)
@@ -354,13 +370,13 @@
     pl.run_scoped(body, *[pltpu.ACC(unit)(shape, jnp.float32) for _ in range(3) for unit in range(2)])
 
 
-def solve(own, cells, table, ham_diag, ham_coup, energies):
+def solve(energy, cells, table, ham_diag, ham_coup):
     slabs, order, _ = ham_diag.shape
     vmem = pl.BlockSpec(memory_space=VMEM)
     return pl.pallas_call(
-        functools.partial(solve_kernel, energies=energies),
+        solve_kernel,
         out_shape=jax.ShapeDtypeStruct((2, slabs, order, order), jnp.float32),
-        in_specs=[pl.BlockSpec(memory_space=SMEM), vmem, vmem, vmem, vmem],
+        in_specs=[vmem] * 5,
         out_specs=pl.BlockSpec(memory_space=pl.ANY),
         scratch_shapes=[
             pltpu.VMEM((slabs, order, 2 * order), jnp.float32),
@@ -369,7 +385,7 @@
         ],
         compiler_params=pltpu.CompilerParams(vmem_limit_bytes=16 * 2**20),
         name="solve",
-    )(own, cells, table, ham_diag, ham_coup)
+    )(energy, cells, table, ham_diag, ham_coup)
 
 
 def on_device(ham_diag, ham_coup, neighbors, pair_count, shifts, g_pairs, emit_coup, absorb_coup):
@@ -387,8 +403,10 @@
     cells = cells.reshape(2, devices, rows_per, LANES).transpose(1, 0, 2, 3)
     cells = cells.reshape(devices, 2 * rows_per, LANES)
     owned = lax.all_to_all(cells, AXES, 0, 0, tiled=True)
-    table, coef = prepare(own, neighbors, pair_count, emit_coup, absorb_coup, slabs, order, rows_per)
-    sigma = convolve(shifts, owned, coef)
+    table, coef, steps, energy = prepare(
+        own, neighbors, pair_count, shifts, emit_coup, absorb_coup, slabs, order, rows_per, devices
+    )
+    sigma = convolve(steps, owned, coef)
     sigma = lax.all_to_all(sigma, AXES, 0, 0, tiled=True)
     lines = 8 * slots // LANES
     if rows_per != lines:
@@ -396,7 +414,7 @@
         sigma = sigma.reshape(2, devices * rows_per, LANES)[:, :rows]
         sigma = sigma.reshape(2, rows // lines, lines, LANES).transpose(1, 0, 2, 3)
         sigma = sigma.reshape(rows // lines, 2 * lines, LANES)
-    green = solve(own, sigma, table, ham_diag, ham_coup, devices)
+    green = solve(energy, sigma, table, ham_diag, ham_coup)
     return green.reshape(2, 1, slabs, order, order)
 
 

time: 38.3 us -> 37.7 us (0.984)
  Pallas kernels: 12.6 us -> 12.1 us
    pallas_call x1, Pallas kernels: 0.87 us -> 0.33 us  [convolve(): pl.pallas_call(convolve_kernel, out_shape=jax.ShapeDtypeStruct(cells.shap...]
where the time goes in v6:
time: 37.7 us; the launch traced here: 37.5 us
  Pallas kernels  12.1 us (32%)
  blocking collectives  10 us (27%)
  starting transfers between devices  7.33 us (19%)
  waiting for transfers between devices  6.34 us (17%)
  local copies, waits for them, and re-layouts  1.59 us (4%)
    all_to_all x1, blocking collectives, on_device(): sigma = lax.all_to_all(sigma, AXES, 0, 0, tiled=True)  10 us
    pallas_call x1, Pallas kernels, solve(): pl.pallas_call(solve_kernel, out_shape=jax.ShapeDtypeStruct((2, slabs, or...  9.94 us
    all_to_all x1, starting transfers between devices, on_device(): owned = lax.all_to_all(cells, AXES, 0, 0, tiled=True)  7.33 us
    all_to_all x1, waiting for transfers between devices, on_device(): owned = lax.all_to_all(cells, AXES, 0, 0, tiled=True)  6.34 us
    pallas_call x1, Pallas kernels, prepare(): pl.pallas_call(functools.partial(prepare_kernel, energies=energies), out_...  1.85 us
    another operation x1, local copies, waits for them, and re-layouts, on_device(): cells = cells.reshape(2, devices, rows_per, LANES).transpose(1, 0, 2, 3)  1.58 us
  transfers between devices with their start and end apart: 1, of which 1 were waited for; matrix products, arithmetic and copies ran while one was open for 0% of the time, Pallas kernels for 5%

profile of v6, /device:TPU:0, one launch (start us, length us, event | category | flops | bytes accessed | tf_op | source)
XLA Modules:
  0.0 37.5 jit_solution(8649411166522098152)
XLA Ops:
  0.0 1.6 %copy.9 = f32[2,32,4,128]{3,2,0,1:T(4,128)} copy(f32[2,32,4,128]{3,2,1,0:T(4,128)} %bitcast.10) | data formatting | bytes 262144 | tf_op jit(solution)/shard_map/reshape;reshape | solution.py:403
  1.6 7.3 %all-to-all-start = ((f32[32,8,128]{2,1,0:T(8,128)}), f32[32,8,128]{2,1,0:T(8,128)S(1)}, u32[]{:S(2)}, u32[]{:S(2)}) async-start(f32[32,8,128]{2,1,0:T(8,128)} %bitcast.5), calls=%async_computation | async-start | bytes 262144 | tf_op jit(solution)/shard_map/all_to_all | solution.py:405
  8.9 1.9 %prepare.1 = (s32[2,128,128]{2,1,0:T(8,128)S(1)}, f32[2,2,8,8,128]{4,3,2,1,0:T(8,128)S(1)}, s32[8,8,128]{2,1,0:T(8,128)S(1)}, f32[8,128]{1,0:T(8,128)S(1)}) custom-call(s32[1]{0:T(128)} %bitcast.own_ref, s32[64,256]{1,0:T(8,128)} %bitcast.11, s32[2,128]{1,0:T(2,128)} %bitcast.12, s32[8]{0:T(128)} %shifts_hbm.1, f32[2,8,16384]{2,1,0:T(8,128)} %emit_hbm.1, ...), custom_call_target="tpu_custom_call" | custom-call | tf_op jit(solution)/shard_map/prepare/pallas_call | solution.py:95
  10.8 6.3 %all-to-all-done.cells_ref = f32[32,8,128]{2,1,0:T(8,128)S(1)} async-done(((f32[32,8,128]{2,1,0:T(8,128)}), f32[32,8,128]{2,1,0:T(8,128)S(1)}, u32[]{:S(2)}, u32[]{:S(2)}) %all-to-all-start) | async-done | bytes 131104 | tf_op jit(solution)/shard_map/all_to_all | solution.py:405
  17.1 0.3 convolve.1
  17.5 0.0 copy-start
  17.5 0.0 copy-start.1
  17.5 10.0 %all_to_all.10.cells_ref = f32[32,8,128]{2,1,0:T(8,128)S(1)} all-to-all(f32[32,8,128]{2,1,0:T(8,128)S(1)} %convolve.1), channel_id=1, replica_groups=mesh['freq'=2,'atom'=16] {'freq','atom'}, dimensions={0} | all-to-all | bytes 262144 | tf_op jit(solution)/shard_map/all_to_all | solution.py:410
  27.5 0.0 copy-done
  27.5 0.0 copy-done.1
  27.5 9.9 %solve.1 = f32[2,2,128,128]{3,2,1,0:T(8,128)} custom-call(f32[8,128]{1,0:T(8,128)S(1)} %get-tuple-element.9.energy_ref, f32[32,8,128]{2,1,0:T(8,128)S(1)} %all_to_all.10.cells_ref, s32[2,128,128]{2,1,0:T(8,128)S(1)} %get-tuple-element.12.table_ref, f32[2,128,128]{2,1,0:T(8,128)S(1)} %copy-done, f32[1,128,128]{2,1,0:T(8,128)S(1)} %copy-done.1), custom_call_target="tpu_custom_call" | custom-call | tf_op jit(solution)/shard_map/solve/pallas_call | solution.py:376
Async XLA Ops:
  1.6 15.5 %all-to-all-start = ((f32[32,8,128]{2,1,0:T(8,128)}), f32[32,8,128]{2,1,0:T(8,128)S(1)}, u32[]{:S(2)}, u32[]{:S(2)}) async-start(f32[32,8,128]{2,1,0:T(8,128)} %bitcast.5), calls=%async_computation | async-start | bytes 262144 | tf_op jit(solution)/shard_map/all_to_all | solution.py:405
  17.5 10.1 %copy-start = (f32[2,128,128]{2,1,0:T(8,128)S(1)}, f32[2,128,128]{2,1,0:T(8,128)}, u32[]{:S(2)}) copy-start(f32[2,128,128]{2,1,0:T(8,128)} %diag_ref.1) | copy-start | bytes 393220
  17.5 10.1 %copy-start.1 = (f32[1,128,128]{2,1,0:T(8,128)S(1)}, f32[1,128,128]{2,1,0:T(8,128)}, u32[]{:S(2)}) copy-start(f32[1,128,128]{2,1,0:T(8,128)} %coup_ref.1) | copy-start | bytes 196612

commit v7 on v6

--- a/solution.py
+++ b/solution.py
@@ -24,12 +24,13 @@
 
 
 def prepare_kernel(
-    own_ref,
+    cells_hbm,
     neighbors_hbm,
     count_hbm,
     shifts_hbm,
     emit_hbm,
     absorb_hbm,
+    cells_ref,
     table_ref,
     coef_ref,
     steps_ref,
@@ -42,11 +43,12 @@
     *,
     energies,
 ):
+    own = lax.axis_index("freq") * lax.axis_size("atom") + lax.axis_index("atom")
     slabs, order, _ = table_ref.shape
     slots = neighbors_ref.shape[0]
     half = coef_ref.shape[3] // 2
     width = half * LANES
-    block = jnp.minimum(own_ref[0], emit_hbm.shape[2] // width - 1)
+    block = jnp.minimum(own, emit_hbm.shape[2] // width - 1)
     lanes = pl.ds(pl.multiple_of(block * width, LANES), width)
     copies = [
         pltpu.make_async_copy(neighbors_hbm, neighbors_ref, sems.at[0]),
@@ -55,9 +57,13 @@
         pltpu.make_async_copy(absorb_hbm.at[:, :, lanes], weights_ref.at[1], sems.at[3]),
         pltpu.make_async_copy(shifts_hbm, shifts_ref, sems.at[4]),
     ]
+    lines = cells_hbm.shape[2]
+    for part in range(cells_hbm.shape[0]):
+        rows = slice(part * lines, (part + 1) * lines)
+        copies.append(pltpu.make_async_copy(cells_hbm.at[part], cells_ref.at[:, rows, :], sems.at[5 + part]))
     for copy in copies:
         copy.start()
-    position = jnp.full(energy_ref.shape, own_ref[0], jnp.int32).astype(jnp.float32)
+    position = jnp.full(energy_ref.shape, own, jnp.int32).astype(jnp.float32)
     energy_ref[...] = ENERGY_LOW + ENERGY_SPAN * position / energies
     copies[0].wait()
     copies[1].wait()
@@ -72,7 +78,7 @@
         for slot in range(slots):
             found = jnp.where(listed[slot : slot + 1, :] == column, slot, found)
         table_ref[slab] = jnp.where(found >= 0, found + offset, -1).T
-    for copy in copies[2:]:
+    for copy in copies[2:5]:
         copy.wait()
     for mode in range(steps_ref.shape[0]):
         steps_ref[mode] = jnp.full(steps_ref.shape[1:], shifts_ref[mode], jnp.int32)
@@ -85,42 +91,36 @@
             coef_ref[side, 0, :, half + row, :] = real
             coef_ref[side, 1, :, row, :] = imag
             coef_ref[side, 1, :, half + row, :] = -imag
-
-
-def prepare(own, neighbors, pair_count, shifts, emit_coup, absorb_coup, slabs, order, rows_per, energies):
+    for copy in copies[5:]:
+        copy.wait()
+
+
+def prepare(cells, neighbors, pair_count, shifts, emit_coup, absorb_coup, slabs, order):
+    parts, devices, rows_per, _ = cells.shape
     modes = emit_coup.shape[1]
     atoms, slots = neighbors.shape
-    arrays = (neighbors.T, pair_count.reshape(slabs, order), shifts, emit_coup, absorb_coup)
-    whole = lambda *shape: pl.BlockSpec(shape, lambda i, own_ref: (0,) * len(shape))
+    arrays = (cells, neighbors.T, pair_count.reshape(slabs, order), shifts, emit_coup, absorb_coup)
     return pl.pallas_call(
-        functools.partial(prepare_kernel, energies=energies),
+        functools.partial(prepare_kernel, energies=devices),
         out_shape=(
+            jax.ShapeDtypeStruct((devices, parts * rows_per, LANES), jnp.float32),
             jax.ShapeDtypeStruct((slabs, order, order), jnp.int32),
             jax.ShapeDtypeStruct((2, 2, modes, 2 * rows_per, LANES), jnp.float32),
             jax.ShapeDtypeStruct((modes, 8, LANES), jnp.int32),
             jax.ShapeDtypeStruct((8, LANES), jnp.float32),
         ),
-        grid_spec=pltpu.PrefetchScalarGridSpec(
-            num_scalar_prefetch=1,
-            grid=(1,),
-            in_specs=[pl.BlockSpec(memory_space=pltpu.HBM)] * 5,
-            out_specs=(
-                whole(slabs, order, order),
-                whole(2, 2, modes, 2 * rows_per, LANES),
-                whole(modes, 8, LANES),
-                whole(8, LANES),
-            ),
-            scratch_shapes=[
-                pltpu.VMEM((slots, atoms), jnp.int32),
-                pltpu.VMEM((slabs, order), jnp.int32),
-                pltpu.SMEM((modes,), jnp.int32),
-                pltpu.VMEM((2, 2, modes, rows_per * LANES), jnp.float32),
-                pltpu.SemaphoreType.DMA((5,)),
-            ],
-        ),
+        in_specs=[pl.BlockSpec(memory_space=pltpu.HBM)] * 6,
+        out_specs=(pl.BlockSpec(memory_space=VMEM),) * 5,
+        scratch_shapes=[
+            pltpu.VMEM((slots, atoms), jnp.int32),
+            pltpu.VMEM((slabs, order), jnp.int32),
+            pltpu.SMEM((modes,), jnp.int32),
+            pltpu.VMEM((2, 2, modes, rows_per * LANES), jnp.float32),
+            pltpu.SemaphoreType.DMA((7,)),
+        ],
         compiler_params=pltpu.CompilerParams(vmem_limit_bytes=16 * 2**20),
         name="prepare",
-    )(own, *[pltpu.with_memory_space_constraint(array, pltpu.HBM) for array in arrays])
+    )(*[pltpu.with_memory_space_constraint(array, pltpu.HBM) for array in arrays])
 
 
 def convolve_kernel(steps_ref, cells_ref, coef_ref, out_ref, padded_ref):
@@ -392,7 +392,6 @@
     slabs, order, _ = ham_diag.shape
     atoms, slots = neighbors.shape
     devices = lax.axis_size("freq") * lax.axis_size("atom")
-    own = (lax.axis_index("freq") * lax.axis_size("atom") + lax.axis_index("atom")).astype(jnp.int32).reshape(1)
     rows = g_pairs.shape[2] // LANES
     rows_per = -(-rows // devices)
     spare = rows_per * devices - rows
@@ -400,12 +399,10 @@
     cells = g_pairs.reshape(2, rows, LANES)
     if spare:
         cells = jnp.pad(cells, ((0, 0), (0, spare), (0, 0)))
-    cells = cells.reshape(2, devices, rows_per, LANES).transpose(1, 0, 2, 3)
-    cells = cells.reshape(devices, 2 * rows_per, LANES)
+    cells, table, coef, steps, energy = prepare(
+        cells.reshape(2, devices, rows_per, LANES), neighbors, pair_count, shifts, emit_coup, absorb_coup, slabs, order
+    )
     owned = lax.all_to_all(cells, AXES, 0, 0, tiled=True)
-    table, coef, steps, energy = prepare(
-        own, neighbors, pair_count, shifts, emit_coup, absorb_coup, slabs, order, rows_per, devices
-    )
     sigma = convolve(steps, owned, coef)
     sigma = lax.all_to_all(sigma, AXES, 0, 0, tiled=True)
     lines = 8 * slots // LANES

time: 37.7 us -> 37.7 us (level)
  blocking collectives: 10 us -> 25.4 us
  starting transfers between devices: 7.33 us -> 0 us
  waiting for transfers between devices: 6.34 us -> 0 us
  local copies, waits for them, and re-layouts: 1.59 us -> 0.01 us
    all_to_all x0 -> x1, blocking collectives: none -> 15.3 us  [on_device(): owned = lax.all_to_all(cells, AXES, 0, 0, tiled=True)]
    all_to_all x1 -> x0, starting transfers between devices: 7.33 us -> none  [on_device(): owned = lax.all_to_all(cells, AXES, 0, 0, tiled=True)]
    all_to_all x1 -> x0, waiting for transfers between devices: 6.34 us -> none  [on_device(): owned = lax.all_to_all(cells, AXES, 0, 0, tiled=True)]
    another operation x1 -> x0, local copies, waits for them, and re-layouts: 1.58 us -> none  [on_device(): cells = cells.reshape(2, devices, rows_per, LANES).transpose(1, 0, 2, 3)]
  transfers between devices with their start and end apart: 1 -> 0, of which waited for: 1 -> 0; matrix products, arithmetic and copies ran while one was open for 0% -> 0% of each run, Pallas kernels for 5% -> 0%
where the time goes in v7:
time: 37.7 us; the launch traced here: 37.5 us
  blocking collectives  25.4 us (67%)
  Pallas kernels  12.1 us (32%)
    all_to_all x1, blocking collectives, on_device(): owned = lax.all_to_all(cells, AXES, 0, 0, tiled=True)  15.3 us
    all_to_all x1, blocking collectives, on_device(): sigma = lax.all_to_all(sigma, AXES, 0, 0, tiled=True)  10 us
    pallas_call x1, Pallas kernels, solve(): pl.pallas_call(solve_kernel, out_shape=jax.ShapeDtypeStruct((2, slabs, or...  9.92 us
    pallas_call x1, Pallas kernels, prepare(): pl.pallas_call(functools.partial(prepare_kernel, energies=devices), out_s...  1.87 us

profile of v7, /device:TPU:0, one launch (start us, length us, event | category | flops | bytes accessed | tf_op | source)
XLA Modules:
  0.0 37.5 jit_solution(7311322888283967479)
XLA Ops:
  0.0 1.9 %prepare.1 = (f32[32,8,128]{2,1,0:T(8,128)S(1)}, s32[2,128,128]{2,1,0:T(8,128)S(1)}, f32[2,2,8,8,128]{4,3,2,1,0:T(8,128)S(1)}, s32[8,8,128]{2,1,0:T(8,128)S(1)}, f32[8,128]{1,0:T(8,128)S(1)}) custom-call(f32[2,32,4,128]{3,2,1,0:T(4,128)} %bitcast.6, s32[64,256]{1,0:T(8,128)} %bitcast.7, s32[2,128]{1,0:T(2,128)} %bitcast.8, s32[8]{0:T(128)} %shifts_hbm.1, ...), custom_call_target="tpu_custom_call" | custom-call | tf_op jit(solution)/shard_map/prepare/pallas_call | solution.py:103
  1.9 15.3 %all_to_all.10.cells_ref = f32[32,8,128]{2,1,0:T(8,128)S(1)} all-to-all(f32[32,8,128]{2,1,0:T(8,128)S(1)} %get-tuple-element.12), channel_id=1, replica_groups=mesh['freq'=2,'atom'=16] {'freq','atom'}, dimensions={0} | all-to-all | bytes 262144 | tf_op jit(solution)/shard_map/all_to_all | solution.py:405
  17.2 0.3 convolve.1
  17.5 0.0 copy-start
  17.6 0.0 copy-start.1
  17.6 10.0 %all_to_all.11.cells_ref = f32[32,8,128]{2,1,0:T(8,128)S(1)} all-to-all(f32[32,8,128]{2,1,0:T(8,128)S(1)} %convolve.1), channel_id=1, replica_groups=mesh['freq'=2,'atom'=16] {'freq','atom'}, dimensions={0} | all-to-all | bytes 262144 | tf_op jit(solution)/shard_map/all_to_all | solution.py:407
  27.6 0.0 copy-done
  27.6 0.0 copy-done.1
  27.6 9.9 %solve.1 = f32[2,2,128,128]{3,2,1,0:T(8,128)} custom-call(f32[8,128]{1,0:T(8,128)S(1)} %get-tuple-element.10.energy_ref, f32[32,8,128]{2,1,0:T(8,128)S(1)} %all_to_all.11.cells_ref, s32[2,128,128]{2,1,0:T(8,128)S(1)} %get-tuple-element.14.table_ref, f32[2,128,128]{2,1,0:T(8,128)S(1)} %copy-done, f32[1,128,128]{2,1,0:T(8,128)S(1)} %copy-done.1), custom_call_target="tpu_custom_call" | custom-call | tf_op jit(solution)/shard_map/solve/pallas_call | solution.py:376
Async XLA Ops:
  17.5 10.1 %copy-start = (f32[2,128,128]{2,1,0:T(8,128)S(1)}, f32[2,128,128]{2,1,0:T(8,128)}, u32[]{:S(2)}) copy-start(f32[2,128,128]{2,1,0:T(8,128)} %diag_ref.1) | copy-start | bytes 393220
  17.6 10.1 %copy-start.1 = (f32[1,128,128]{2,1,0:T(8,128)S(1)}, f32[1,128,128]{2,1,0:T(8,128)}, u32[]{:S(2)}) copy-start(f32[1,128,128]{2,1,0:T(8,128)} %coup_ref.1) | copy-start | bytes 196612

commit v8 on v7

--- a/solution.py
+++ b/solution.py
@@ -21,6 +21,20 @@
 AXES = ("freq", "atom")
 VMEM = pltpu.MemorySpace.VMEM
 SMEM = pltpu.MemorySpace.SMEM
+
+
+def lanes_of(listed):
+    slots, order = listed.shape
+    column = lax.broadcasted_iota(jnp.int32, (order, order), 0).astype(jnp.float32).astype(jnp.bfloat16)
+    column = column.reshape(order // 16, 16, order)
+    found = jnp.full((order // 16, 16, order), -1.0, jnp.bfloat16)
+    for slot in range(slots):
+        row = jnp.broadcast_to(listed[slot : slot + 1, :], (16, order)).astype(jnp.bfloat16)
+        found = jnp.where(row[None] == column, jnp.bfloat16(slot), found)
+    found = found.reshape(order, order).astype(jnp.float32).astype(jnp.int32)
+    lane = lax.broadcasted_iota(jnp.int32, (order, order), 1)
+    offset = lax.rem(lane, LANES // slots) * slots
+    return jnp.where(found >= 0, found + offset, -1).T
 
 
 def prepare_kernel(
@@ -31,6 +45,7 @@
     emit_hbm,
     absorb_hbm,
     cells_ref,
+    listed_ref,
     table_ref,
     coef_ref,
     steps_ref,
@@ -44,8 +59,7 @@
     energies,
 ):
     own = lax.axis_index("freq") * lax.axis_size("atom") + lax.axis_index("atom")
-    slabs, order, _ = table_ref.shape
-    slots = neighbors_ref.shape[0]
+    slabs, slots, order = listed_ref.shape
     half = coef_ref.shape[3] // 2
     width = half * LANES
     block = jnp.minimum(own, emit_hbm.shape[2] // width - 1)
@@ -68,16 +82,10 @@
     copies[0].wait()
     copies[1].wait()
     slot_id = lax.broadcasted_iota(jnp.int32, (slots, order), 0)
-    column = lax.broadcasted_iota(jnp.int32, (order, order), 0)
-    lane = lax.broadcasted_iota(jnp.int32, (order, order), 1)
-    offset = lax.rem(lane, LANES // slots) * slots
     for slab in range(slabs):
         listed = neighbors_ref[:, slab * order : (slab + 1) * order]
-        listed = jnp.where(slot_id < count_ref[slab : slab + 1, :], listed, -1)
-        found = jnp.full((order, order), -1, jnp.int32)
-        for slot in range(slots):
-            found = jnp.where(listed[slot : slot + 1, :] == column, slot, found)
-        table_ref[slab] = jnp.where(found >= 0, found + offset, -1).T
+        listed_ref[slab] = jnp.where(slot_id < count_ref[slab : slab + 1, :], listed, -1).astype(jnp.float32)
+    table_ref[...] = lanes_of(listed_ref[slabs - 1])
     for copy in copies[2:5]:
         copy.wait()
     for mode in range(steps_ref.shape[0]):
@@ -104,13 +112,14 @@
         functools.partial(prepare_kernel, energies=devices),
         out_shape=(
             jax.ShapeDtypeStruct((devices, parts * rows_per, LANES), jnp.float32),
-            jax.ShapeDtypeStruct((slabs, order, order), jnp.int32),
+            jax.ShapeDtypeStruct((slabs, slots, order), jnp.float32),
+            jax.ShapeDtypeStruct((order, order), jnp.int32),
             jax.ShapeDtypeStruct((2, 2, modes, 2 * rows_per, LANES), jnp.float32),
             jax.ShapeDtypeStruct((modes, 8, LANES), jnp.int32),
             jax.ShapeDtypeStruct((8, LANES), jnp.float32),
         ),
         in_specs=[pl.BlockSpec(memory_space=pltpu.HBM)] * 6,
-        out_specs=(pl.BlockSpec(memory_space=VMEM),) * 5,
+        out_specs=(pl.BlockSpec(memory_space=VMEM),) * 6,
         scratch_shapes=[
             pltpu.VMEM((slots, atoms), jnp.int32),
             pltpu.VMEM((slabs, order), jnp.int32),
@@ -221,19 +230,19 @@
 
     def feed(self, stage, *rows):
         for block, left in rows:
-            half = left.shape[0] // 2
             for unit in range(2):
+                mine = [left[row : row + 16] for row in range(16 * unit, left.shape[0], 32)]
                 pltpu.matmul_acc_lhs(
                     self.blocks[block][unit],
-                    left[unit * half : (unit + 1) * half],
+                    jnp.concatenate(mine, axis=0),
                     load_staged_rhs=stage,
                 )
             stage = None
 
     def take(self, block):
-        return jnp.concatenate(
-            [pltpu.matmul_pop(self.blocks[block][unit]) for unit in range(2)], axis=0
-        )
+        halves = [pltpu.matmul_pop(self.blocks[block][unit]) for unit in range(2)]
+        rows = range(0, halves[0].shape[0], 16)
+        return jnp.concatenate([half[row : row + 16] for row in rows for half in halves], axis=0)
 
     def product(self, left, right, transpose=False):
         for index, factor in enumerate(right):
@@ -252,11 +261,14 @@
     for index in range(count):
         narrow = y.astype(jnp.bfloat16)
         stage = mxu.load(embed(narrow))
-        mxu.feed(stage, (0, narrow))
+        more = index + 1 < count
+        if more:
+            mxu.feed(stage, (0, narrow))
         if index:
             x = (x - mxu.take(1)) + x
-        mxu.feed(None, (1, x.astype(jnp.bfloat16)))
-        y = (y - mxu.take(0)) + y
+        mxu.feed(None if more else stage, (1, x.astype(jnp.bfloat16)))
+        if more:
+            y = (y - mxu.take(0)) + y
     x = (x - mxu.take(1)) + x
 
     high, low = pieces(x, 2)
@@ -297,7 +309,7 @@
     return jnp.take_along_axis(values, index, axis=axis, mode="promise_in_bounds")
 
 
-def solve_kernel(energy_ref, cells_ref, table_ref, diag_ref, coup_ref, out_ref, matrix_ref, stage_ref, sems):
+def solve_kernel(energy_ref, cells_ref, listed_ref, table_ref, diag_ref, coup_ref, out_ref, matrix_ref, stage_ref, sems):
     slabs, order, _ = diag_ref.shape
     unit = unit_pair(order)
     energy = energy_ref[...]
@@ -305,11 +317,11 @@
     lines = cells_ref.shape[1] // 2
     line_of = row // (8 // lines)
 
-    def assemble(slab):
+    def assemble(slab, lanes):
         for block in range(order // 8):
             cell = cells_ref[slab * (order // 8) + block]
             rows = slice(block * 8, block * 8 + 8)
-            table = table_ref[slab, rows, :]
+            table = lanes[rows, :]
             held = table >= 0
             lane = jnp.where(held, table, 0)
             for part in range(2):
@@ -322,7 +334,7 @@
                     entry = BROADEN * eye - sigma
                 matrix_ref[slab, rows, part * order : (part + 1) * order] = entry
 
-    assemble(1)
+    assemble(1, table_ref[...])
     coup = coup_ref[0]
     none = jnp.zeros_like(coup)
     coup_left = jnp.concatenate([coup, none], axis=1)
@@ -342,7 +354,7 @@
         mxu = Multiplier([accumulators[2 * i : 2 * i + 2] for i in range(3)])
         right = pieces(coup_right, 2)
         last, left_of, last_norm = iterate(mxu, matrix_ref[1], pieces(coup_left, 2), INV_STEPS - EXACT_STEPS)
-        assemble(0)
+        assemble(0, lanes_of(listed_ref[0]))
         matrix = matrix_ref[0] - mxu.product(pieces(left_of, 2), right)
         right_of = mxu.product(pieces(last, 2), right)
         first, both, first_norm = iterate(mxu, matrix, pieces(right_of, 2), INV_STEPS - EXACT_STEPS)
@@ -370,13 +382,13 @@
     pl.run_scoped(body, *[pltpu.ACC(unit)(shape, jnp.float32) for _ in range(3) for unit in range(2)])
 
 
-def solve(energy, cells, table, ham_diag, ham_coup):
+def solve(energy, cells, listed, table, ham_diag, ham_coup):
     slabs, order, _ = ham_diag.shape
     vmem = pl.BlockSpec(memory_space=VMEM)
     return pl.pallas_call(
         solve_kernel,
         out_shape=jax.ShapeDtypeStruct((2, slabs, order, order), jnp.float32),
-        in_specs=[vmem] * 5,
+        in_specs=[vmem] * 6,
         out_specs=pl.BlockSpec(memory_space=pl.ANY),
         scratch_shapes=[
             pltpu.VMEM((slabs, order, 2 * order), jnp.float32),
@@ -385,7 +397,7 @@
         ],
         compiler_params=pltpu.CompilerParams(vmem_limit_bytes=16 * 2**20),
         name="solve",
-    )(energy, cells, table, ham_diag, ham_coup)
+    )(energy, cells, listed, table, ham_diag, ham_coup)
 
 
 def on_device(ham_diag, ham_coup, neighbors, pair_count, shifts, g_pairs, emit_coup, absorb_coup):
@@ -399,7 +411,7 @@
     cells = g_pairs.reshape(2, rows, LANES)
     if spare:
         cells = jnp.pad(cells, ((0, 0), (0, spare), (0, 0)))
-    cells, table, coef, steps, energy = prepare(
+    cells, listed, table, coef, steps, energy = prepare(
         cells.reshape(2, devices, rows_per, LANES), neighbors, pair_count, shifts, emit_coup, absorb_coup, slabs, order
     )
     owned = lax.all_to_all(cells, AXES, 0, 0, tiled=True)
@@ -411,7 +423,7 @@
         sigma = sigma.reshape(2, devices * rows_per, LANES)[:, :rows]
         sigma = sigma.reshape(2, rows // lines, lines, LANES).transpose(1, 0, 2, 3)
         sigma = sigma.reshape(rows // lines, 2 * lines, LANES)
-    green = solve(energy, sigma, table, ham_diag, ham_coup)
+    green = solve(energy, sigma, listed, table, ham_diag, ham_coup)
     return green.reshape(2, 1, slabs, order, order)
 
 

time: 37.7 us -> 36.8 us (0.976)
  Pallas kernels: 12.1 us -> 11.2 us
    pallas_call x1, Pallas kernels: 1.87 us -> 1.25 us  [prepare(): pl.pallas_call(functools.partial(prepare_kernel, energies=devices), out_s...]
where the time goes in v8:
time: 36.8 us; the launch traced here: 36.6 us
  blocking collectives  25.4 us (69%)
  Pallas kernels  11.2 us (30%)
    all_to_all x1, blocking collectives, on_device(): owned = lax.all_to_all(cells, AXES, 0, 0, tiled=True)  15.3 us
    all_to_all x1, blocking collectives, on_device(): sigma = lax.all_to_all(sigma, AXES, 0, 0, tiled=True)  10 us
    pallas_call x1, Pallas kernels, solve(): pl.pallas_call(solve_kernel, out_shape=jax.ShapeDtypeStruct((2, slabs, or...  9.57 us
    pallas_call x1, Pallas kernels, prepare(): pl.pallas_call(functools.partial(prepare_kernel, energies=devices), out_s...  1.25 us

profile of v8, /device:TPU:0, one launch (start us, length us, event | category | flops | bytes accessed | tf_op | source)
XLA Modules:
  0.0 36.6 jit_solution(17566614346305593158)
XLA Ops:
  0.0 1.3 %prepare.1 = (f32[32,8,128]{2,1,0:T(8,128)S(1)}, f32[2,64,128]{2,1,0:T(8,128)S(1)}, s32[128,128]{1,0:T(8,128)S(1)}, f32[2,2,8,8,128]{4,3,2,1,0:T(8,128)S(1)}, s3...) custom-call(f32[2,32,4,128]{3,2,1,0:T(4,128)} %bitcast.6, s32[64,256]{1,0:T(8,128)} %bitcast.7, s32[2,128]{1,0:T(2,128)} %bitcast.8, ...), custom_call_target="tpu_custom_call" | custom-call | tf_op jit(solution)/shard_map/prepare/pallas_call | solution.py:111
  1.3 15.3 %all_to_all.10.cells_ref = f32[32,8,128]{2,1,0:T(8,128)S(1)} all-to-all(f32[32,8,128]{2,1,0:T(8,128)S(1)} %get-tuple-element.13), channel_id=1, replica_groups=mesh['freq'=2,'atom'=16] {'freq','atom'}, dimensions={0} | all-to-all | bytes 262144 | tf_op jit(solution)/shard_map/all_to_all | solution.py:417
  16.6 0.3 convolve.1
  16.9 0.0 copy-start
  16.9 0.0 copy-start.1
  17.0 10.0 %all_to_all.11.cells_ref = f32[32,8,128]{2,1,0:T(8,128)S(1)} all-to-all(f32[32,8,128]{2,1,0:T(8,128)S(1)} %convolve.1), channel_id=1, replica_groups=mesh['freq'=2,'atom'=16] {'freq','atom'}, dimensions={0} | all-to-all | bytes 262144 | tf_op jit(solution)/shard_map/all_to_all | solution.py:419
  27.0 0.0 copy-done
  27.0 0.0 copy-done.1
  27.0 9.6 %solve.1 = f32[2,2,128,128]{3,2,1,0:T(8,128)} custom-call(f32[8,128]{1,0:T(8,128)S(1)} %get-tuple-element.11.energy_ref, f32[32,8,128]{2,1,0:T(8,128)S(1)} %all_to_all.11.cells_ref, f32[2,64,128]{2,1,0:T(8,128)S(1)} %get-tuple-element.15.listed_ref, s32[128,128]{1,0:T(8,128)S(1)} %get-tuple-element.16.table_ref, f32[2,128,128]{2,1,0:T(8,128)S(1)} %copy-done, ...), custom_call_target="tpu_custom_call" | custom-call | tf_op jit(solution)/shard_map/solve/pallas_call | solution.py:388
Async XLA Ops:
  16.9 10.1 %copy-start = (f32[2,128,128]{2,1,0:T(8,128)S(1)}, f32[2,128,128]{2,1,0:T(8,128)}, u32[]{:S(2)}) copy-start(f32[2,128,128]{2,1,0:T(8,128)} %diag_ref.1) | copy-start | bytes 393220
  16.9 10.1 %copy-start.1 = (f32[1,128,128]{2,1,0:T(8,128)S(1)}, f32[1,128,128]{2,1,0:T(8,128)}, u32[]{:S(2)}) copy-start(f32[1,128,128]{2,1,0:T(8,128)} %coup_ref.1) | copy-start | bytes 196612

commit v9 on v8

--- a/solution.py
+++ b/solution.py
@@ -265,11 +265,11 @@
         if more:
             mxu.feed(stage, (0, narrow))
         if index:
-            x = (x - mxu.take(1)) + x
+            x = (x + x) - mxu.take(1)
         mxu.feed(None if more else stage, (1, x.astype(jnp.bfloat16)))
         if more:
-            y = (y - mxu.take(0)) + y
-    x = (x - mxu.take(1)) + x
+            y = (y + y) - mxu.take(0)
+    x = (x + x) - mxu.take(1)
 
     high, low = pieces(x, 2)
     wide = mxu.load(embed(high))

time: 36.8 us -> 36.6 us (level)
  no operation moved by 1% of the time
where the time goes in v9:
time: 36.6 us; the launch traced here: 36.4 us
  blocking collectives  25.4 us (69%)
  Pallas kernels  11 us (30%)
    all_to_all x1, blocking collectives, on_device(): owned = lax.all_to_all(cells, AXES, 0, 0, tiled=True)  15.3 us
    all_to_all x1, blocking collectives, on_device(): sigma = lax.all_to_all(sigma, AXES, 0, 0, tiled=True)  10 us
    pallas_call x1, Pallas kernels, solve(): pl.pallas_call(solve_kernel, out_shape=jax.ShapeDtypeStruct((2, slabs, or...  9.42 us
    pallas_call x1, Pallas kernels, prepare(): pl.pallas_call(functools.partial(prepare_kernel, energies=devices), out_s...  1.25 us

profile of v9, /device:TPU:0, one launch (start us, length us, event | category | flops | bytes accessed | tf_op | source)
XLA Modules:
  0.0 36.4 jit_solution(18074576529756399706)
XLA Ops:
  0.0 1.3 %prepare.1 = (f32[32,8,128]{2,1,0:T(8,128)S(1)}, f32[2,64,128]{2,1,0:T(8,128)S(1)}, s32[128,128]{1,0:T(8,128)S(1)}, f32[2,2,8,8,128]{4,3,2,1,0:T(8,128)S(1)}, s3...) custom-call(f32[2,32,4,128]{3,2,1,0:T(4,128)} %bitcast.6, s32[64,256]{1,0:T(8,128)} %bitcast.7, s32[2,128]{1,0:T(2,128)} %bitcast.8, ...), custom_call_target="tpu_custom_call" | custom-call | tf_op jit(solution)/shard_map/prepare/pallas_call | solution.py:111
  1.3 15.3 %all_to_all.10.cells_ref = f32[32,8,128]{2,1,0:T(8,128)S(1)} all-to-all(f32[32,8,128]{2,1,0:T(8,128)S(1)} %get-tuple-element.13), channel_id=1, replica_groups=mesh['freq'=2,'atom'=16] {'freq','atom'}, dimensions={0} | all-to-all | bytes 262144 | tf_op jit(solution)/shard_map/all_to_all | solution.py:417
  16.6 0.3 convolve.1
  16.9 0.0 copy-start
  16.9 0.0 copy-start.1
  17.0 10.0 %all_to_all.11.cells_ref = f32[32,8,128]{2,1,0:T(8,128)S(1)} all-to-all(f32[32,8,128]{2,1,0:T(8,128)S(1)} %convolve.1), channel_id=1, replica_groups=mesh['freq'=2,'atom'=16] {'freq','atom'}, dimensions={0} | all-to-all | bytes 262144 | tf_op jit(solution)/shard_map/all_to_all | solution.py:419
  27.0 0.0 copy-done
  27.0 0.0 copy-done.1
  27.0 9.4 %solve.1 = f32[2,2,128,128]{3,2,1,0:T(8,128)} custom-call(f32[8,128]{1,0:T(8,128)S(1)} %get-tuple-element.11.energy_ref, f32[32,8,128]{2,1,0:T(8,128)S(1)} %all_to_all.11.cells_ref, f32[2,64,128]{2,1,0:T(8,128)S(1)} %get-tuple-element.15.listed_ref, s32[128,128]{1,0:T(8,128)S(1)} %get-tuple-element.16.table_ref, f32[2,128,128]{2,1,0:T(8,128)S(1)} %copy-done, ...), custom_call_target="tpu_custom_call" | custom-call | tf_op jit(solution)/shard_map/solve/pallas_call | solution.py:388
Async XLA Ops:
  16.9 10.1 %copy-start = (f32[2,128,128]{2,1,0:T(8,128)S(1)}, f32[2,128,128]{2,1,0:T(8,128)}, u32[]{:S(2)}) copy-start(f32[2,128,128]{2,1,0:T(8,128)} %diag_ref.1) | copy-start | bytes 393220
  16.9 10.1 %copy-start.1 = (f32[1,128,128]{2,1,0:T(8,128)S(1)}, f32[1,128,128]{2,1,0:T(8,128)}, u32[]{:S(2)}) copy-start(f32[1,128,128]{2,1,0:T(8,128)} %coup_ref.1) | copy-start | bytes 196612

commit v10 on v9

--- a/solution.py
+++ b/solution.py
@@ -79,13 +79,6 @@
         copy.start()
     position = jnp.full(energy_ref.shape, own, jnp.int32).astype(jnp.float32)
     energy_ref[...] = ENERGY_LOW + ENERGY_SPAN * position / energies
-    copies[0].wait()
-    copies[1].wait()
-    slot_id = lax.broadcasted_iota(jnp.int32, (slots, order), 0)
-    for slab in range(slabs):
-        listed = neighbors_ref[:, slab * order : (slab + 1) * order]
-        listed_ref[slab] = jnp.where(slot_id < count_ref[slab : slab + 1, :], listed, -1).astype(jnp.float32)
-    table_ref[...] = lanes_of(listed_ref[slabs - 1])
     for copy in copies[2:5]:
         copy.wait()
     for mode in range(steps_ref.shape[0]):
@@ -99,6 +92,13 @@
             coef_ref[side, 0, :, half + row, :] = real
             coef_ref[side, 1, :, row, :] = imag
             coef_ref[side, 1, :, half + row, :] = -imag
+    copies[0].wait()
+    copies[1].wait()
+    slot_id = lax.broadcasted_iota(jnp.int32, (slots, order), 0)
+    for slab in range(slabs):
+        listed = neighbors_ref[:, slab * order : (slab + 1) * order]
+        listed_ref[slab] = jnp.where(slot_id < count_ref[slab : slab + 1, :], listed, -1).astype(jnp.float32)
+    table_ref[...] = lanes_of(listed_ref[slabs - 1])
     for copy in copies[5:]:
         copy.wait()
 

time: 36.6 us -> 36.6 us (level)
  no operation moved by 1% of the time
where the time goes in v10:
time: 36.6 us; the launch traced here: 36.4 us
  blocking collectives  25.4 us (69%)
  Pallas kernels  11 us (30%)
    all_to_all x1, blocking collectives, on_device(): owned = lax.all_to_all(cells, AXES, 0, 0, tiled=True)  15.3 us
    all_to_all x1, blocking collectives, on_device(): sigma = lax.all_to_all(sigma, AXES, 0, 0, tiled=True)  10 us
    pallas_call x1, Pallas kernels, solve(): pl.pallas_call(solve_kernel, out_shape=jax.ShapeDtypeStruct((2, slabs, or...  9.43 us
    pallas_call x1, Pallas kernels, prepare(): pl.pallas_call(functools.partial(prepare_kernel, energies=devices), out_s...  1.23 us

profile of v10, /device:TPU:0, one launch (start us, length us, event | category | flops | bytes accessed | tf_op | source)
XLA Modules:
  0.0 36.4 jit_solution(9794004890277368861)
XLA Ops:
  0.0 1.2 %prepare.1 = (f32[32,8,128]{2,1,0:T(8,128)S(1)}, f32[2,64,128]{2,1,0:T(8,128)S(1)}, s32[128,128]{1,0:T(8,128)S(1)}, f32[2,2,8,8,128]{4,3,2,1,0:T(8,128)S(1)}, s3...) custom-call(f32[2,32,4,128]{3,2,1,0:T(4,128)} %bitcast.6, s32[64,256]{1,0:T(8,128)} %bitcast.7, s32[2,128]{1,0:T(2,128)} %bitcast.8, ...), custom_call_target="tpu_custom_call" | custom-call | tf_op jit(solution)/shard_map/prepare/pallas_call | solution.py:111
  1.2 15.3 %all_to_all.10.cells_ref = f32[32,8,128]{2,1,0:T(8,128)S(1)} all-to-all(f32[32,8,128]{2,1,0:T(8,128)S(1)} %get-tuple-element.13), channel_id=1, replica_groups=mesh['freq'=2,'atom'=16] {'freq','atom'}, dimensions={0} | all-to-all | bytes 262144 | tf_op jit(solution)/shard_map/all_to_all | solution.py:417
  16.6 0.3 convolve.1
  16.9 0.0 copy-start
  16.9 0.0 copy-start.1
  16.9 10.0 %all_to_all.11.cells_ref = f32[32,8,128]{2,1,0:T(8,128)S(1)} all-to-all(f32[32,8,128]{2,1,0:T(8,128)S(1)} %convolve.1), channel_id=1, replica_groups=mesh['freq'=2,'atom'=16] {'freq','atom'}, dimensions={0} | all-to-all | bytes 262144 | tf_op jit(solution)/shard_map/all_to_all | solution.py:419
  27.0 0.0 copy-done
  27.0 0.0 copy-done.1
  27.0 9.4 %solve.1 = f32[2,2,128,128]{3,2,1,0:T(8,128)} custom-call(f32[8,128]{1,0:T(8,128)S(1)} %get-tuple-element.11.energy_ref, f32[32,8,128]{2,1,0:T(8,128)S(1)} %all_to_all.11.cells_ref, f32[2,64,128]{2,1,0:T(8,128)S(1)} %get-tuple-element.15.listed_ref, s32[128,128]{1,0:T(8,128)S(1)} %get-tuple-element.16.table_ref, f32[2,128,128]{2,1,0:T(8,128)S(1)} %copy-done, ...), custom_call_target="tpu_custom_call" | custom-call | tf_op jit(solution)/shard_map/solve/pallas_call | solution.py:388
Async XLA Ops:
  16.9 10.1 %copy-start = (f32[2,128,128]{2,1,0:T(8,128)S(1)}, f32[2,128,128]{2,1,0:T(8,128)}, u32[]{:S(2)}) copy-start(f32[2,128,128]{2,1,0:T(8,128)} %diag_ref.1) | copy-start | bytes 393220
  16.9 10.1 %copy-start.1 = (f32[1,128,128]{2,1,0:T(8,128)S(1)}, f32[1,128,128]{2,1,0:T(8,128)}, u32[]{:S(2)}) copy-start(f32[1,128,128]{2,1,0:T(8,128)} %coup_ref.1) | copy-start | bytes 196612

commit v11 on v9

--- a/solution.py
+++ b/solution.py
@@ -46,7 +46,6 @@
     absorb_hbm,
     cells_ref,
     listed_ref,
-    table_ref,
     coef_ref,
     steps_ref,
     energy_ref,
@@ -85,7 +84,6 @@
     for slab in range(slabs):
         listed = neighbors_ref[:, slab * order : (slab + 1) * order]
         listed_ref[slab] = jnp.where(slot_id < count_ref[slab : slab + 1, :], listed, -1).astype(jnp.float32)
-    table_ref[...] = lanes_of(listed_ref[slabs - 1])
     for copy in copies[2:5]:
         copy.wait()
     for mode in range(steps_ref.shape[0]):
@@ -113,13 +111,12 @@
         out_shape=(
             jax.ShapeDtypeStruct((devices, parts * rows_per, LANES), jnp.float32),
             jax.ShapeDtypeStruct((slabs, slots, order), jnp.float32),
-            jax.ShapeDtypeStruct((order, order), jnp.int32),
             jax.ShapeDtypeStruct((2, 2, modes, 2 * rows_per, LANES), jnp.float32),
             jax.ShapeDtypeStruct((modes, 8, LANES), jnp.int32),
             jax.ShapeDtypeStruct((8, LANES), jnp.float32),
         ),
         in_specs=[pl.BlockSpec(memory_space=pltpu.HBM)] * 6,
-        out_specs=(pl.BlockSpec(memory_space=VMEM),) * 6,
+        out_specs=(pl.BlockSpec(memory_space=VMEM),) * 5,
         scratch_shapes=[
             pltpu.VMEM((slots, atoms), jnp.int32),
             pltpu.VMEM((slabs, order), jnp.int32),
@@ -132,7 +129,8 @@
     )(*[pltpu.with_memory_space_constraint(array, pltpu.HBM) for array in arrays])
 
 
-def convolve_kernel(steps_ref, cells_ref, coef_ref, out_ref, padded_ref):
+def convolve_kernel(steps_ref, cells_ref, coef_ref, listed_ref, out_ref, table_ref, padded_ref):
+    table_ref[...] = lanes_of(listed_ref[listed_ref.shape[0] - 1])
     energies, height, _ = cells_ref.shape
     modes = coef_ref.shape[2]
     half = height // 2
@@ -170,18 +168,21 @@
     lax.fori_loop(0, energies // group, combine, 0, unroll=energies // group <= 2)
 
 
-def convolve(steps, cells, coef):
+def convolve(steps, cells, coef, listed):
     energies, height, _ = cells.shape
     vmem = pl.BlockSpec(memory_space=VMEM)
     return pl.pallas_call(
         convolve_kernel,
-        out_shape=jax.ShapeDtypeStruct(cells.shape, jnp.float32),
-        in_specs=[vmem, vmem, vmem],
-        out_specs=vmem,
+        out_shape=(
+            jax.ShapeDtypeStruct(cells.shape, jnp.float32),
+            jax.ShapeDtypeStruct((listed.shape[2],) * 2, jnp.int32),
+        ),
+        in_specs=[vmem] * 4,
+        out_specs=(vmem, vmem),
         scratch_shapes=[pltpu.VMEM((energies + 2 * HALO, height, LANES), jnp.float32)],
         compiler_params=pltpu.CompilerParams(vmem_limit_bytes=16 * 2**20),
         name="convolve",
-    )(steps, cells, coef)
+    )(steps, cells, coef, listed)
 
 
 def embed(pair):
@@ -411,11 +412,11 @@
     cells = g_pairs.reshape(2, rows, LANES)
     if spare:
         cells = jnp.pad(cells, ((0, 0), (0, spare), (0, 0)))
-    cells, listed, table, coef, steps, energy = prepare(
+    cells, listed, coef, steps, energy = prepare(
         cells.reshape(2, devices, rows_per, LANES), neighbors, pair_count, shifts, emit_coup, absorb_coup, slabs, order
     )
     owned = lax.all_to_all(cells, AXES, 0, 0, tiled=True)
-    sigma = convolve(steps, owned, coef)
+    sigma, table = convolve(steps, owned, coef, listed)
     sigma = lax.all_to_all(sigma, AXES, 0, 0, tiled=True)
     lines = 8 * slots // LANES
     if rows_per != lines:

time: 36.6 us -> 36.5 us (level)
  no operation moved by 1% of the time
where the time goes in v11:
time: 36.5 us; the launch traced here: 36.3 us
  blocking collectives  25.4 us (70%)
  Pallas kernels  10.9 us (30%)
    all_to_all x1, blocking collectives, on_device(): owned = lax.all_to_all(cells, AXES, 0, 0, tiled=True)  15.3 us
    all_to_all x1, blocking collectives, on_device(): sigma = lax.all_to_all(sigma, AXES, 0, 0, tiled=True)  10 us
    pallas_call x1, Pallas kernels, solve(): pl.pallas_call(solve_kernel, out_shape=jax.ShapeDtypeStruct((2, slabs, or...  9.44 us
    pallas_call x1, Pallas kernels, prepare(): pl.pallas_call(functools.partial(prepare_kernel, energies=devices), out_s...  1.02 us

profile of v11, /device:TPU:0, one launch (start us, length us, event | category | flops | bytes accessed | tf_op | source)
XLA Modules:
  0.0 36.3 jit_solution(3022802461759267872)
XLA Ops:
  0.0 1.0 %prepare.1 = (f32[32,8,128]{2,1,0:T(8,128)S(1)}, f32[2,64,128]{2,1,0:T(8,128)S(1)}, f32[2,2,8,8,128]{4,3,2,1,0:T(8,128)S(1)}, s32[8,8,128]{2,1,0:T(8,128)S(1)}, f32[8,128]{1,0:T(8,128)S(1)}) custom-call(f32[2,32,4,128]{3,2,1,0:T(4,128)} %bitcast.6, s32[64,256]{1,0:T(8,128)} %bitcast.7, s32[2,128]{1,0:T(2,128)} %bitcast.8, s32[8]{0:T(128)} %shifts_hbm.1, ...), custom_call_target="tpu_custom_call" | custom-call | tf_op jit(solution)/shard_map/prepare/pallas_call | solution.py:109
  1.0 15.3 %all_to_all.10.cells_ref = f32[32,8,128]{2,1,0:T(8,128)S(1)} all-to-all(f32[32,8,128]{2,1,0:T(8,128)S(1)} %get-tuple-element.14), channel_id=1, replica_groups=mesh['freq'=2,'atom'=16] {'freq','atom'}, dimensions={0} | all-to-all | bytes 262144 | tf_op jit(solution)/shard_map/all_to_all | solution.py:418
  16.4 0.5 %convolve.1 = (f32[32,8,128]{2,1,0:T(8,128)S(1)}, s32[128,128]{1,0:T(8,128)S(1)}) custom-call(s32[8,8,128]{2,1,0:T(8,128)S(1)} %get-tuple-element.13.steps_ref, f32[32,8,128]{2,1,0:T(8,128)S(1)} %all_to_all.10.cells_ref, f32[2,2,8,8,128]{4,3,2,1,0:T(8,128)S(1)} %get-tuple-element.15.coef_ref, f32[2,64,128]{2,1,0:T(8,128)S(1)} %get-tuple-element.16.listed_ref), custom_call_target="tpu_custom_call" | custom-call | tf_op jit(solution)/shard_map/convolve/pallas_call | solution.py:174
  16.8 0.0 copy-start
  16.8 0.0 copy-start.1
  16.8 10.0 %all_to_all.11.cells_ref = f32[32,8,128]{2,1,0:T(8,128)S(1)} all-to-all(f32[32,8,128]{2,1,0:T(8,128)S(1)} %get-tuple-element.17), channel_id=1, replica_groups=mesh['freq'=2,'atom'=16] {'freq','atom'}, dimensions={0} | all-to-all | bytes 262144 | tf_op jit(solution)/shard_map/all_to_all | solution.py:420
  26.9 0.0 copy-done
  26.9 0.0 copy-done.1
  26.9 9.4 %solve.1 = f32[2,2,128,128]{3,2,1,0:T(8,128)} custom-call(f32[8,128]{1,0:T(8,128)S(1)} %get-tuple-element.12.energy_ref, f32[32,8,128]{2,1,0:T(8,128)S(1)} %all_to_all.11.cells_ref, f32[2,64,128]{2,1,0:T(8,128)S(1)} %get-tuple-element.16.listed_ref, s32[128,128]{1,0:T(8,128)S(1)} %get-tuple-element.18.table_ref, f32[2,128,128]{2,1,0:T(8,128)S(1)} %copy-done, ...), custom_call_target="tpu_custom_call" | custom-call | tf_op jit(solution)/shard_map/solve/pallas_call | solution.py:389
Async XLA Ops:
  16.8 10.1 %copy-start = (f32[2,128,128]{2,1,0:T(8,128)S(1)}, f32[2,128,128]{2,1,0:T(8,128)}, u32[]{:S(2)}) copy-start(f32[2,128,128]{2,1,0:T(8,128)} %diag_ref.1) | copy-start | bytes 393220
  16.8 10.1 %copy-start.1 = (f32[1,128,128]{2,1,0:T(8,128)S(1)}, f32[1,128,128]{2,1,0:T(8,128)}, u32[]{:S(2)}) copy-start(f32[1,128,128]{2,1,0:T(8,128)} %coup_ref.1) | copy-start | bytes 196612

commit v12 on v11

--- a/solution.py
+++ b/solution.py
@@ -261,7 +261,10 @@
     y = product * scale
     for index in range(count):
         narrow = y.astype(jnp.bfloat16)
-        stage = mxu.load(embed(narrow))
+        turned = (-y[:, order:]).astype(jnp.bfloat16)
+        stage = mxu.load(
+            jnp.concatenate([narrow, jnp.concatenate([turned, narrow[:, :order]], axis=1)], axis=0)
+        )
         more = index + 1 < count
         if more:
             mxu.feed(stage, (0, narrow))

time: 36.5 us -> 36.5 us (level)
  no operation moved by 1% of the time
where the time goes in v12:
time: 36.5 us; the launch traced here: 36.3 us
  blocking collectives  25.4 us (70%)
  Pallas kernels  10.9 us (30%)
    all_to_all x1, blocking collectives, on_device(): owned = lax.all_to_all(cells, AXES, 0, 0, tiled=True)  15.3 us
    all_to_all x1, blocking collectives, on_device(): sigma = lax.all_to_all(sigma, AXES, 0, 0, tiled=True)  10 us
    pallas_call x1, Pallas kernels, solve(): pl.pallas_call(solve_kernel, out_shape=jax.ShapeDtypeStruct((2, slabs, or...  9.43 us
    pallas_call x1, Pallas kernels, prepare(): pl.pallas_call(functools.partial(prepare_kernel, energies=devices), out_s...  1.02 us

profile of v12, /device:TPU:0, one launch (start us, length us, event | category | flops | bytes accessed | tf_op | source)
XLA Modules:
  0.0 36.3 jit_solution(13301696890618262211)
XLA Ops:
  0.0 1.0 %prepare.1 = (f32[32,8,128]{2,1,0:T(8,128)S(1)}, f32[2,64,128]{2,1,0:T(8,128)S(1)}, f32[2,2,8,8,128]{4,3,2,1,0:T(8,128)S(1)}, s32[8,8,128]{2,1,0:T(8,128)S(1)}, f32[8,128]{1,0:T(8,128)S(1)}) custom-call(f32[2,32,4,128]{3,2,1,0:T(4,128)} %bitcast.6, s32[64,256]{1,0:T(8,128)} %bitcast.7, s32[2,128]{1,0:T(2,128)} %bitcast.8, s32[8]{0:T(128)} %shifts_hbm.1, ...), custom_call_target="tpu_custom_call" | custom-call | tf_op jit(solution)/shard_map/prepare/pallas_call | solution.py:109
  1.0 15.3 %all_to_all.10.cells_ref = f32[32,8,128]{2,1,0:T(8,128)S(1)} all-to-all(f32[32,8,128]{2,1,0:T(8,128)S(1)} %get-tuple-element.14), channel_id=1, replica_groups=mesh['freq'=2,'atom'=16] {'freq','atom'}, dimensions={0} | all-to-all | bytes 262144 | tf_op jit(solution)/shard_map/all_to_all | solution.py:421
  16.4 0.5 %convolve.1 = (f32[32,8,128]{2,1,0:T(8,128)S(1)}, s32[128,128]{1,0:T(8,128)S(1)}) custom-call(s32[8,8,128]{2,1,0:T(8,128)S(1)} %get-tuple-element.13.steps_ref, f32[32,8,128]{2,1,0:T(8,128)S(1)} %all_to_all.10.cells_ref, f32[2,2,8,8,128]{4,3,2,1,0:T(8,128)S(1)} %get-tuple-element.15.coef_ref, f32[2,64,128]{2,1,0:T(8,128)S(1)} %get-tuple-element.16.listed_ref), custom_call_target="tpu_custom_call" | custom-call | tf_op jit(solution)/shard_map/convolve/pallas_call | solution.py:174
  16.8 0.0 copy-start
  16.8 0.0 copy-start.1
  16.8 10.0 %all_to_all.11.cells_ref = f32[32,8,128]{2,1,0:T(8,128)S(1)} all-to-all(f32[32,8,128]{2,1,0:T(8,128)S(1)} %get-tuple-element.17), channel_id=1, replica_groups=mesh['freq'=2,'atom'=16] {'freq','atom'}, dimensions={0} | all-to-all | bytes 262144 | tf_op jit(solution)/shard_map/all_to_all | solution.py:423
  26.9 0.0 copy-done
  26.9 0.0 copy-done.1
  26.9 9.4 %solve.1 = f32[2,2,128,128]{3,2,1,0:T(8,128)} custom-call(f32[8,128]{1,0:T(8,128)S(1)} %get-tuple-element.12.energy_ref, f32[32,8,128]{2,1,0:T(8,128)S(1)} %all_to_all.11.cells_ref, f32[2,64,128]{2,1,0:T(8,128)S(1)} %get-tuple-element.16.listed_ref, s32[128,128]{1,0:T(8,128)S(1)} %get-tuple-element.18.table_ref, f32[2,128,128]{2,1,0:T(8,128)S(1)} %copy-done, ...), custom_call_target="tpu_custom_call" | custom-call | tf_op jit(solution)/shard_map/solve/pallas_call | solution.py:392
Async XLA Ops:
  16.8 10.1 %copy-start = (f32[2,128,128]{2,1,0:T(8,128)S(1)}, f32[2,128,128]{2,1,0:T(8,128)}, u32[]{:S(2)}) copy-start(f32[2,128,128]{2,1,0:T(8,128)} %diag_ref.1) | copy-start | bytes 393220
  16.8 10.1 %copy-start.1 = (f32[1,128,128]{2,1,0:T(8,128)S(1)}, f32[1,128,128]{2,1,0:T(8,128)}, u32[]{:S(2)}) copy-start(f32[1,128,128]{2,1,0:T(8,128)} %coup_ref.1) | copy-start | bytes 196612
